TPU v7x, 128 devices: a whole 4x4x4 slice. The times are simulated.
128 devices in a mesh: leaf: 4 (over y), row: 4 (over z), col: 8 (over x, core).
Axes of the slice: x: 4, y: 4, z: 4, core: 2. Of those that a mesh axis runs over, the one named last changes fastest.
Arguments:
- rhs_leaf: bfloat16 [4, 12288, 256], P('leaf', 'col'), may hold values from -6 to 6
- rhs_parent: bfloat16 [16384, 256], P(('leaf', 'row', 'col')), may hold values from -6 to 6
- inv_leaf: bfloat16 [4, 12288, 12288], P('leaf', 'row', 'col'), as said below
- panel: bfloat16 [4, 6144, 12288], P('leaf', 'col', 'row'), may hold values from -0.0546875 to 0.0546875
- row_map: int32 [4, 6144], P('leaf', 'col'), may hold values from 0 to 16383, as said below
- inv_parent: bfloat16 [16384, 16384], P(('row', 'col'), 'leaf'), as said below
Outputs:
- sol_leaf: bfloat16 [4, 12288, 256], P('leaf', 'col')
- sol_parent: bfloat16 [16384, 256], P(('leaf', 'row', 'col'))
Inputs may be any that keep to these rules, and one draw needn't show every extreme that they name: Within one leaf the 6144 entries of row_map are distinct parent rows. Split the parent rows into 128 owner blocks of 16384 // 128 consecutive rows: in each aligned block of 192 consecutive entries of a leaf, at most 2 entries fall in one owner block, and exactly 2 in some. `inv_leaf`: lower triangular: zeros above the diagonal, diagonal entries between 0.5 and 2. `inv_parent`: lower triangular: zeros above the diagonal, diagonal entries between 0.5 and 2.
All inputs are finite; a program needn't handle non-finite values.
Results may differ from a plain program's by a relative error of at most 0.01.
Values may be sent and summed in bfloat16 or wider, within the bound.
A program may use at most 128 MiB of HBM per device.

v0:
```python
import jax
import jax.numpy as jnp
from jax import lax
from jax.sharding import PartitionSpec as P


def dense_updates(update, row_map, rhs_parent):
    total_rows = rhs_parent.shape[0] * lax.axis_size(("leaf", "row", "col"))
    dense = jnp.zeros((total_rows, rhs_parent.shape[1]), jnp.float32)
    dense = dense.at[row_map[0]].add(-update)
    offset = lax.axis_index(("leaf", "row", "col")) * rhs_parent.shape[0]
    own_rows = lax.dynamic_slice_in_dim(dense, offset, rhs_parent.shape[0], 0) + rhs_parent.astype(
        jnp.float32
    )
    return lax.dynamic_update_slice_in_dim(dense, own_rows, offset, 0)


def per_device(rhs_leaf, rhs_parent, inv_leaf, panel, row_map, inv_parent):
    leaf_part = jnp.dot(inv_leaf[0], rhs_leaf[0], preferred_element_type=jnp.float32)
    forward = lax.psum(leaf_part, "col").astype(jnp.bfloat16)
    update = jnp.dot(panel[0], forward, preferred_element_type=jnp.float32)
    dense = dense_updates(update, row_map, rhs_parent)
    leaf_block = lax.psum_scatter(dense, "leaf", scatter_dimension=0, tiled=True)
    reduced = lax.psum(leaf_block, ("row", "col")).astype(jnp.bfloat16)
    parent_part = jnp.dot(inv_parent, reduced, preferred_element_type=jnp.float32)
    fwd_parent = lax.psum(parent_part, "leaf").astype(jnp.bfloat16)
    back_part = lax.dot_general(
        inv_parent, fwd_parent, (((0,), (0,)), ((), ())), preferred_element_type=jnp.float32
    )
    sol_parent = lax.psum_scatter(
        back_part, ("row", "col"), scatter_dimension=0, tiled=True
    ).astype(jnp.bfloat16)
    whole_parent = lax.all_gather(sol_parent, ("leaf", "row", "col"), axis=0, tiled=True)
    picked = jnp.take(whole_parent, row_map[0], axis=0)
    coupling_part = lax.dot_general(
        panel[0], picked, (((0,), (0,)), ((), ())), preferred_element_type=jnp.float32
    )
    coupling = lax.psum(coupling_part, "col")
    corrected = (forward.astype(jnp.float32) - coupling).astype(jnp.bfloat16)
    final_part = lax.dot_general(
        inv_leaf[0], corrected, (((0,), (0,)), ((), ())), preferred_element_type=jnp.float32
    )
    sol_leaf = lax.psum(final_part, "row").astype(jnp.bfloat16)
    return (sol_leaf[None], sol_parent)


def solution(mesh):
    in_specs = (
        P("leaf", "col", None),
        P(("leaf", "row", "col"), None),
        P("leaf", "row", "col"),
        P("leaf", "col", "row"),
        P("leaf", "col"),
        P(("row", "col"), "leaf"),
    )
    out_specs = (P("leaf", "col", None), P(("leaf", "row", "col"), None))
    return jax.shard_map(
        per_device, mesh=mesh, in_specs=in_specs, out_specs=out_specs, check_vma=False
    )
```

profile of v0, /device:TPU:1, one launch (start us, length us, event | category | flops | bytes accessed | tf_op | source)
XLA Modules:
  0.0 722.6 jit_solution(5863380692495050478)
XLA Ops:
  7.2 0.0 copy-start
  7.2 0.0 reduce-scatter.3.cloned.1.call-start
  7.2 1.1 copy-done
  8.3 8.0 %fusion.2 = f32[3072,256]{1,0:T(8,128)} fusion(bf16[1,3072,1536]{2,1,0:T(8,128)(2,1)} %param.8, bf16[1,1536,256]{2,1,0:T(8,128)(2,1)S(1)} %copy-done), kind=kOutput, calls=%fused_computation.4 | convolution fusion | flops 2415919104 | bytes 13369344 | tf_op jit(solution)/shard_map/dot_general | solution.py:19
  16.3 54.8 %all-reduce.7 = bf16[3072,256]{1,0:T(8,128)(2,1)S(1)} all-reduce(f32[3072,256]{1,0:T(8,128)} %fusion.2), channel_id=1, replica_groups=mesh['leaf'=4,'row'=4,'col'=8] {'col'}, use_global_device_ids=true, to_apply=%region_0.0 | all-reduce | flops 786432 | bytes 4718592 | tf_op jit(solution)/shard_map/psum | solution.py:20
  71.0 0.0 copy-start.4
  71.0 3.8 fusion.21
  74.8 0.3 copy.12
  75.1 0.0 copy-done.4
  75.1 0.0 copy-start.3
  75.1 12.3 %scatter_custom_fusion = f32[16384,256]{1,0:T(8,128)} fusion(s32[768]{0:T(1024)S(1)} %fusion.34, f32[768,256]{1,0:T(8,128)S(1)} %copy.12, f32[]{:T(128)} %constant.14.clone.1), kind=kCustom, calls=%fused_computation.6 | custom fusion | flops 196608 | bytes 16777220 | tf_op jit(solution)/shard_map/scatter-add | solution.py:10
  87.4 0.0 copy-done.3
  87.4 1.6 add_dynamic-update-slice_fusion
  89.0 0.0 reduce-scatter.3.cloned.1.call-update
  89.0 0.0 reduce-scatter.5.cloned.1.call-start
  89.1 151.1 %reduce-scatter.3.cloned.1.call-done = f32[4096,256]{1,0:T(8,128)} async-done(((f32[16384,256]{1,0:T(8,128)}), f32[4096,256]{1,0:T(8,128)}) %reduce-scatter.3.cloned.1.call-update) | async-done | bytes 4194320 | tf_op jit(solution)/shard_map/reduce_scatter | solution.py:23
  240.1 147.9 %all-reduce.8 = bf16[4096,256]{1,0:T(8,128)(2,1)} all-reduce(f32[4096,256]{1,0:T(8,128)} %reduce-scatter.3.cloned.1.call-done), channel_id=1, replica_groups=mesh['leaf'=4,'row'=4,'col'=8] {'row','col'}, use_global_device_ids=true, to_apply=%region_3.0 | all-reduce | flops 1048576 | bytes 6291456 | tf_op jit(solution)/shard_map/psum | solution.py:24
  388.1 4.1 fusion.24
  392.2 17.5 %all-reduce.9 = bf16[512,256]{0,1:T(8,128)(2,1)S(1)} all-reduce(f32[512,256]{0,1:T(8,128)S(1)} %fusion.24), channel_id=1, replica_groups=mesh['leaf'=4,'row'=4,'col'=8] {'leaf'}, use_global_device_ids=true, to_apply=%region_4.0 | all-reduce | flops 131072 | bytes 786432 | tf_op jit(solution)/shard_map/psum | solution.py:26
  409.7 5.4 convolution_bitcast_fusion
  415.1 0.0 reduce-scatter.5.cloned.1.call-update
  415.1 0.0 all-gather.2.cloned.1.call-start
  415.1 84.0 %reduce-scatter.5.cloned.1.call-done = f32[128,256]{0,1:T(8,128)} async-done(((f32[4096,256]{0,1:T(8,128)}), f32[128,256]{0,1:T(8,128)}) %reduce-scatter.5.cloned.1.call-update) | async-done | bytes 131088 | tf_op jit(solution)/shard_map/reduce_scatter | solution.py:30
  499.1 1.5 convert_element_type.29
  500.7 0.0 all-gather.2.cloned.1.call-update
  500.7 0.0 all-reduce.6.cloned.1.call-start
  500.8 82.3 %all-gather.2.cloned.1.call-done = bf16[16384,256]{0,1:T(8,128)(2,1)} async-done(((bf16[128,256]{0,1:T(8,128)(2,1)}), bf16[16384,256]{0,1:T(8,128)(2,1)}) %all-gather.2.cloned.1.call-update) | async-done | bytes 8388624 | tf_op jit(solution)/shard_map/all_gather | solution.py:33
  583.1 11.9 %copy.13 = bf16[16384,256]{1,0:T(8,128)(2,1)} copy(bf16[16384,256]{0,1:T(8,128)(2,1)} %all-gather.2.cloned.1.call-done) | data formatting | bytes 16777216 | tf_op jit(solution)/shard_map/all_gather | solution.py:33
  594.9 6.6 gather_fusion
  601.5 0.0 copy-start.2
  601.5 6.1 fusion.10
  607.7 0.0 all-reduce.6.cloned.1.call-update
  607.7 0.0 copy-done.2
  607.7 0.7 copy.15
  608.4 65.8 %all-reduce.6.cloned.1.call-done = f32[3072,256]{1,0:T(8,128)} async-done(((f32[3072,256]{1,0:T(8,128)}), f32[3072,256]{1,0:T(8,128)}) %all-reduce.6.cloned.1.call-update) | async-done | bytes 3145744 | tf_op jit(solution)/shard_map/psum | solution.py:38
  674.2 0.0 copy-start.1
  674.2 8.5 %fusion.13 = f32[1536,256]{0,1:T(8,128)} fusion(bf16[1,3072,1536]{2,1,0:T(8,128)(2,1)} %param.8, f32[3072,256]{1,0:T(8,128)} %all-reduce.6.cloned.1.call-done, bf16[3072,256]{1,0:T(8,128)(2,1)S(1)} %all-reduce.7), kind=kOutput, calls=%fused_computation.15 | convolution fusion | flops 2418278400 | bytes 15728640 | tf_op jit(solution)/shard_map/dot_general | solution.py:40
  682.6 32.3 %all-reduce.10 = bf16[1536,256]{0,1:T(8,128)(2,1)S(1)} all-reduce(f32[1536,256]{0,1:T(8,128)} %fusion.13), channel_id=1, replica_groups=mesh['leaf'=4,'row'=4,'col'=8] {'row'}, use_global_device_ids=true, to_apply=%region_7.8 | all-reduce | flops 393216 | bytes 2359296 | tf_op jit(solution)/shard_map/psum | solution.py:43
  715.0 1.2 copy.14
  716.1 0.0 copy-done.1
  (4 shorter events, 0.0 us)
Async XLA Ops:
  7.2 1.1 copy-start
  7.2 233.0 %reduce-scatter.3.cloned.1.call-start = ((), (), s32[]{:S(2)}) async-start(), calls=%async_computation.2 | async-start | bytes 20971520 | tf_op jit(solution)/shard_map/reduce_scatter | solution.py:23
  71.0 4.1 copy-start.4
  75.1 12.3 %copy-start.3 = (bf16[128,256]{1,0:T(8,128)(2,1)S(1)}, bf16[128,256]{1,0:T(8,128)(2,1)}, u32[]{:S(2)}) copy-start(bf16[128,256]{1,0:T(8,128)(2,1)} %param.7) | copy-start | bytes 196612
  89.0 410.1 %reduce-scatter.5.cloned.1.call-start = ((), (), s32[]{:S(2)}) async-start(), calls=%async_computation.3 | async-start | bytes 4325376 | tf_op jit(solution)/shard_map/reduce_scatter | solution.py:30
  415.1 168.0 %all-gather.2.cloned.1.call-start = ((), (), s32[]{:S(2)}) async-start(), calls=%async_computation.4 | async-start | bytes 8454144 | tf_op jit(solution)/shard_map/all_gather | solution.py:33
  500.7 173.5 %all-reduce.6.cloned.1.call-start = ((), (), s32[]{:S(2)}) async-start(), calls=%async_computation.5 | async-start | bytes 6291456 | tf_op jit(solution)/shard_map/psum | solution.py:38
  601.5 6.2 copy-start.2
  674.2 41.9 %copy-start.1 = (bf16[1,1536,256]{2,1,0:T(8,128)(2,1)S(1)}, bf16[1,1536,256]{2,1,0:T(8,128)(2,1)}, u32[]{:S(2)}) copy-start(bf16[1,1536,256]{2,1,0:T(8,128)(2,1)} %param.6) | copy-start | bytes 2359300
Sparse Core Ops, SparseCore 0:
  89.1 150.9 reduce-scatter.2
  415.2 83.8 reduce-scatter.4
  502.5 80.5 all-gather.1
  607.8 66.3 all-reduce.5
where the time goes:
time: 729 us; the launch traced here: 723 us
  waiting for transfers between devices  383 us (53%)
  blocking collectives  252 us (35%)
  matrix products  35.8 us (5%)
  local copies, waits for them, and re-layouts  21.7 us (3%)
  other arithmetic  15.4 us (2%)
  between operations  13.9 us (2%)
    reduce_scatter x1, waiting for transfers between devices, per_device(): lax.psum_scatter(dense, 'leaf', scatter_dimension=0, tiled=True)  151 us
    psum x1, blocking collectives, per_device(): reduced = lax.psum(leaf_block, ('row', 'col')).astype(jnp.bfloat16)  148 us
    reduce_scatter x1, waiting for transfers between devices, per_device(): lax.psum_scatter(back_part, ('row', 'col'), scatter_dimension=0, tiled=True)  84 us
    all_gather x1, waiting for transfers between devices, per_device(): lax.all_gather(sol_parent, ('leaf', 'row', 'col'), axis=0, tiled=True)  82.3 us
    psum x1, waiting for transfers between devices, per_device(): coupling = lax.psum(coupling_part, 'col')  65.8 us
    psum x1, blocking collectives, per_device(): forward = lax.psum(leaf_part, 'col').astype(jnp.bfloat16)  54.8 us
    psum x1, blocking collectives, per_device(): sol_leaf = lax.psum(final_part, 'row').astype(jnp.bfloat16)  32.3 us
    psum x1, blocking collectives, per_device(): fwd_parent = lax.psum(parent_part, 'leaf').astype(jnp.bfloat16)  17.5 us
  transfers between devices with their start and end apart: 4, of which 4 were waited for; matrix products, arithmetic and copies ran while one was open for 0% of the time, Pallas kernels for 0%

commit v1 on v0

v1 whole, which is shorter than its diff:
```python
import jax
import jax.numpy as jnp
from jax import lax
from jax.experimental import pallas as pl
from jax.experimental.pallas import tpu as pltpu
from jax.sharding import PartitionSpec as P

MESH = pl.DeviceIdType.MESH
BF = jnp.bfloat16
F32 = jnp.float32


def dot(a, b):
    return jnp.dot(a, b, preferred_element_type=F32)


class Comm:
    def __init__(self, ssem, rsem):
        self.ssem, self.rsem, self.n, self.sent = ssem, rsem, 0, []
        self.l, self.r, self.c = (lax.axis_index(a) for a in ("leaf", "row", "col"))
        self.x, self.k = self.c // 2, self.c % 2

    def at(self, axis, delta):
        if axis == "x":
            return (self.l, self.r, ((self.x + delta + 4) % 4) * 2 + self.k)
        if axis == "z":
            return (self.l, (self.r + delta + 4) % 4, self.c)
        if axis == "y":
            return ((self.l + delta + 4) % 4, self.r, self.c)
        return (self.l, self.r, self.x * 2 + 1 - self.k)

    def make(self, src, dst, device):
        at = self.n
        self.n += 1
        return pltpu.make_async_remote_copy(
            src_ref=src,
            dst_ref=dst,
            send_sem=self.ssem.at[at],
            recv_sem=self.rsem.at[at],
            device_id=device,
            device_id_type=MESH,
        )

    def send(self, src, dst, axis, delta=0):
        copy = self.make(src, dst, self.at(axis, delta))
        copy.start()
        self.sent.append(copy)
        return copy

    def drain(self):
        for copy in self.sent:
            copy.wait_send()
        self.sent = []


class RingSum:
    def __init__(self, comm, axis, q, slot):
        self.comm, self.axis, self.q, self.slot = comm, axis, q, slot

    def far(self):
        send, q, slot, axis = self.comm.send, self.q, self.slot, self.axis
        self.c0 = send(q(2, 0), slot(0), axis, 1)
        self.c1 = send(q(2, 1), slot(1), axis, -1)

    def near(self):
        send, q, slot, axis = self.comm.send, self.q, self.slot, self.axis
        self.c5 = send(q(1, 1), slot(5), axis, 1)
        self.c4 = send(q(3, 0), slot(4), axis, -1)

    def relay(self):
        send, q, slot, axis = self.comm.send, self.q, self.slot, self.axis
        self.c0.wait_recv()
        q(1, 0)[...] = (q(1, 0)[...].astype(F32) + slot(0)[...].astype(F32)).astype(BF)
        self.c2 = send(q(1, 0), slot(2), axis, 1)
        self.c1.wait_recv()
        q(3, 1)[...] = (q(3, 1)[...].astype(F32) + slot(1)[...].astype(F32)).astype(BF)
        self.c3 = send(q(3, 1), slot(3), axis, -1)

    def total(self, own0, own1):
        slot = self.slot
        self.c4.wait_recv()
        self.c2.wait_recv()
        a = own0 + slot(4)[...].astype(F32) + slot(2)[...].astype(F32)
        self.c5.wait_recv()
        self.c3.wait_recv()
        b = own1 + slot(5)[...].astype(F32) + slot(3)[...].astype(F32)
        return a, b

    def run(self):
        self.far()
        self.near()
        self.relay()


class RingGather:
    def __init__(self, comm, axis, me, g):
        self.comm, self.axis, self.me, self.g = comm, axis, me, g
        send = comm.send
        self.a_up = send(g(me, 0), g(me, 0), axis, 1)
        self.b_dn = send(g(me, 1), g(me, 1), axis, -1)
        self.b_up = send(g(me, 1), g(me, 1), axis, 1)
        self.a_dn = send(g(me, 0), g(me, 0), axis, -1)
        self.prev, self.next, self.opp = (me + 3) % 4, (me + 1) % 4, (me + 2) % 4

    def relay(self):
        send, g = self.comm.send, self.g
        self.a_up.wait_recv()
        self.a_far = send(g(self.prev, 0), g(self.prev, 0), self.axis, 1)
        self.b_dn.wait_recv()
        self.b_far = send(g(self.next, 1), g(self.next, 1), self.axis, -1)

    def near(self):
        self.b_up.wait_recv()
        self.a_dn.wait_recv()

    def far(self):
        self.a_far.wait_recv()
        self.b_far.wait_recv()

    def run(self):
        self.relay()
        self.near()
        self.far()


def kernel(
    x_hbm, rp_hbm, a_hbm, b_hbm, p_hbm, rm_ref,
    out_ref, solp_ref,
    a_v, b_v, p_v, x_v, rp_v,
    sb1, rb1, q1, own1, rr1, y_v, yt,
    u_acc, q2, rr2,
    g_v, r1_v, r2_v, qs, qr, t1, t1t, s1, s1t,
    q3, rr3, gred, q4, rr4, ft,
    sb5, rb5, q5, own5, rz0, rx0, rx1, rz1,
    sp, pk, sb7, rb7, q7, own7, rr7, ct,
    acc8, q8, rr8,
    ssem, rsem, lsem, asem, bsem,
):
    cm = Comm(ssem, rsem)
    l, r, c, x, k = cm.l, cm.r, cm.c, cm.x, cm.k
    me = r * 8 + c
    n8 = y_v.shape[2]
    R = x_v.shape[1]
    H = R // 2
    own = rp_v.shape[0]
    blk = s1t.shape[0]

    loads = [pltpu.make_async_copy(x_hbm, x_v, lsem.at[0])]
    for i, d in enumerate((2, 3, 1, 0)):
        for j, core in enumerate((1 - k, k)):
            rows = pl.ds(pl.multiple_of((((x + d) % 4) * 2 + core) * n8, n8), n8)
            loads.append(pltpu.make_async_copy(a_hbm.at[rows], a_v.at[rows], lsem.at[1 + 2 * i + j]))
    loads.append(pltpu.make_async_copy(rp_hbm, rp_v, lsem.at[9]))
    loads.append(pltpu.make_async_copy(b_hbm, b_v, lsem.at[10]))
    loads.append(pltpu.make_async_copy(p_hbm, p_v, lsem.at[11]))
    for load in loads:
        load.start()

    barrier = pltpu.get_barrier_semaphore()

    def greet(n, _):
        to = (me + n) % 32
        pl.semaphore_signal(barrier, inc=1, device_id=(l, to // 8, to % 8), device_id_type=MESH)
        return 0

    lax.fori_loop(1, 32, greet, 0)
    for d in (1, 3):
        pl.semaphore_signal(barrier, inc=1, device_id=((l + d) % 4, r, c), device_id_type=MESH)

    shift = own.bit_length() - 1
    e = rm_ref[pl.ds(r, 1), :]
    owner = lax.shift_right_logical(e, shift)
    local = lax.bitwise_and(e, own - 1).astype(F32)
    across = jnp.broadcast_to(owner.astype(F32), (blk, blk))
    down = across.T
    before = lax.broadcasted_iota(jnp.int32, (blk, blk), 0) < lax.broadcasted_iota(jnp.int32, (blk, blk), 1)
    rank = jnp.sum(jnp.where((across == down) & before, 1.0, 0.0), axis=0, keepdims=True)
    place = lax.bitwise_and(owner, 31) * 8 + lax.shift_right_logical(owner, 5) * 2
    place = place.astype(F32) + rank
    pick = jnp.where(
        lax.broadcasted_iota(jnp.int32, (256, blk), 0).astype(F32) == jnp.broadcast_to(place, (256, blk)), 1.0, 0.0
    )
    s1[...] = pick.astype(BF)
    s1t[...] = pick.T.astype(BF)
    qv = jnp.sum(pick * jnp.broadcast_to(local + 1.0, (256, blk)), axis=1, keepdims=True)
    qs[...] = jnp.broadcast_to(qv, (256, own)).reshape(32, 8, own)
    qr[pl.ds(me, 1)] = qs[pl.ds(me, 1)]

    pl.semaphore_wait(barrier, 33)

    def plane_exchange(src, dst, which):
        def one(n, _):
            to = (me + n) % 32
            pltpu.make_async_remote_copy(
                src_ref=src.at[to], dst_ref=dst.at[me], send_sem=asem.at[which], recv_sem=bsem.at[which],
                device_id=(l, to // 8, to % 8), device_id_type=MESH,
            ).start()
            return 0

        lax.fori_loop(1, 32, one, 0)

    def plane_wait(src, dst, which):
        copy = pltpu.make_async_remote_copy(
            src_ref=src.at[pl.ds(0, 31)], dst_ref=dst.at[pl.ds(0, 31)], send_sem=asem.at[which],
            recv_sem=bsem.at[which], device_id=cm.at("c", 0), device_id_type=MESH,
        )
        copy.wait_send()
        copy.wait_recv()

    plane_exchange(qs, qr, 0)

    loads[0].wait()
    xv = x_v[...]
    half = n8 // 2
    sib = {}

    def a_rows(d, core):
        return pl.ds(pl.multiple_of((((x + d) % 4) * 2 + core) * n8, n8), n8)

    ring = RingSum(cm, "x", lambda d, h: q1.at[d, pl.ds(h * half, half)], lambda i: rr1.at[i])
    for i, d in enumerate((2, 3, 1, 0)):
        loads[1 + 2 * i].wait()
        sb1[d] = dot(a_v[a_rows(d, 1 - k), :], xv).astype(BF)
        sib[d] = cm.send(sb1.at[d], rb1.at[d], "c")
    for i, d in enumerate((2, 3, 1, 0)):
        loads[2 + 2 * i].wait()
        part = dot(a_v[a_rows(d, k), :], xv)
        sib[d].wait_recv()
        part = part + rb1[d].astype(F32)
        if d:
            q1[d] = part.astype(BF)
        else:
            own1[...] = part
        if d == 2:
            ring.far()
        if d == 1:
            ring.near()
    ring.relay()
    a, b = ring.total(own1[:half], own1[half:])
    y_v[x, k, :half] = a.astype(BF)
    y_v[x, k, half:] = b.astype(BF)

    gat = RingGather(cm, "x", x, lambda i, h: y_v.at[i, k, pl.ds(h * half, half)])
    fwd = [cm.send(y_v.at[x, k], y_v.at[x, k], "c")]
    yt[:, :half] = a.T.astype(BF)
    yt[:, half:] = b.T.astype(BF)
    loads[10].wait()

    def panel_cols(xx, core):
        return pl.ds(pl.multiple_of((xx * 2 + core) * n8, n8), n8)

    def push(xx, core, first=False):
        part = dot(b_v[:, panel_cols(xx, core)], y_v[xx, core])
        u_acc[...] = part if first else u_acc[...] + part

    push(x, k, True)
    gat.relay()
    gat.near()
    fwd.append(cm.send(y_v.at[gat.prev, k], y_v.at[gat.prev, k], "c"))
    fwd.append(cm.send(y_v.at[gat.next, k], y_v.at[gat.next, k], "c"))
    fwd[0].wait_recv()
    push(x, 1 - k)
    push(gat.prev, k)
    push(gat.next, k)
    gat.far()
    fwd.append(cm.send(y_v.at[gat.opp, k], y_v.at[gat.opp, k], "c"))
    fwd[1].wait_recv()
    push(gat.prev, 1 - k)
    fwd[2].wait_recv()
    push(gat.next, 1 - k)
    push(gat.opp, k)
    fwd[3].wait_recv()
    push(gat.opp, 1 - k)

    plane_wait(qs, qr, 0)
    seen = qr[...].reshape(256, own)
    lane = lax.broadcasted_iota(jnp.int32, (256, own), 1).astype(F32) + 1.0
    leaf_of = lax.bitwise_and(
        lax.shift_right_logical(lax.broadcasted_iota(jnp.int32, (256, own), 0), 1), 3
    )
    for i in range(4):
        table = jnp.where((seen == lane) & (leaf_of == i), 1.0, 0.0)
        t1t[:, i * own : (i + 1) * own] = table.astype(BF)
        t1[i * own : (i + 1) * own, :] = table.T.astype(BF)

    quarter = blk // 2

    def u_rows(d):
        return u_acc[pl.ds(pl.multiple_of(((r + d) % 4) * blk, blk), blk), :]

    for d in (2, 1, 3):
        q2[d] = u_rows(d).astype(BF)
    ring = RingSum(cm, "z", lambda d, h: q2.at[d, pl.ds(h * quarter, quarter)], lambda i: rr2.at[i])
    ring.run()
    mine = u_rows(0)
    a, b = ring.total(mine[:quarter], mine[quarter:])
    q2[0, :quarter] = a.astype(BF)
    q2[0, quarter:] = b.astype(BF)

    g_v[...] = dot(s1[...], q2[0]).reshape(32, 8, R)
    r1_v[pl.ds(me, 1)] = g_v[pl.ds(me, 1)]
    plane_exchange(g_v, r1_v, 1)
    plane_wait(g_v, r1_v, 1)
    got = r1_v[...].reshape(256, R).astype(BF)
    hown = own // 2

    def t_rows(d):
        return t1[pl.ds(pl.multiple_of(((l + d) % 4) * own, own), own), :]

    for d in (2, 1, 3):
        q3[d] = dot(t_rows(d), got).astype(BF)
    ring = RingSum(cm, "y", lambda d, h: q3.at[d, pl.ds(h * hown, hown)], lambda i: rr3.at[i])
    ring.far()
    ring.near()
    mine = dot(t_rows(0), got)
    ring.relay()
    a, b = ring.total(mine[:hown], mine[hown:])
    loads[9].wait()
    rp = rp_v[...].astype(F32)
    for h in range(2):
        cols = slice(h * H, (h + 1) * H)
        gred[h, r, x, k, :hown] = (rp[:hown, cols] - a[:, cols]).astype(BF)
        gred[h, r, x, k, hown:] = (rp[hown:, cols] - b[:, cols]).astype(BF)

    g0 = RingGather(cm, "x", x, lambda i, h: gred.at[0, r, i, k, pl.ds(h * hown, hown)])
    g1 = RingGather(cm, "z", r, lambda i, h: gred.at[1, i, x, k, pl.ds(h * hown, hown)])
    g0.relay()
    g1.relay()
    g0.near()
    g0.far()
    g1.near()
    g1.far()
    g2 = RingGather(cm, "z", r, lambda i, h: gred.at[0, i, pl.ds(2 * h, 2), k])
    g3 = RingGather(cm, "x", x, lambda i, h: gred.at[1, pl.ds(2 * h, 2), i, k])
    fwd = [cm.send(gred.at[0, r, :, k], gred.at[0, r, :, k], "c")]
    fwd.append(cm.send(gred.at[1, :, x, k], gred.at[1, :, x, k], "c"))
    g2.relay()
    g3.relay()
    g2.near()
    fwd += [cm.send(gred.at[0, i, :, k], gred.at[0, i, :, k], "c") for i in (g2.prev, g2.next)]
    g3.near()
    fwd += [cm.send(gred.at[1, :, i, k], gred.at[1, :, i, k], "c") for i in (g3.prev, g3.next)]
    g2.far()
    fwd.append(cm.send(gred.at[0, g2.opp, :, k], gred.at[0, g2.opp, :, k], "c"))
    g3.far()
    fwd.append(cm.send(gred.at[1, :, g3.opp, k], gred.at[1, :, g3.opp, k], "c"))
    for copy in fwd:
        copy.wait_recv()

    loads[11].wait()
    parent = None
    for i in range(4):
        rhs = jnp.concatenate([gred[h, i].reshape(8 * own, H) for h in range(2)], axis=1)
        part = dot(p_v[:, i * 8 * own : (i + 1) * 8 * own], rhs)
        parent = part if parent is None else parent + part
    u_acc[: 4 * own] = parent

    def f_rows(d):
        return u_acc[pl.ds(pl.multiple_of(((l + d) % 4) * own, own), own), :]

    for d in (2, 1, 3):
        q4[d] = f_rows(d).astype(BF)
    ring = RingSum(cm, "y", lambda d, h: q4.at[d, pl.ds(h * hown, hown)], lambda i: rr4.at[i])
    ring.run()
    mine = f_rows(0)
    a, b = ring.total(mine[:hown], mine[hown:])
    fp = jnp.concatenate([a, b], axis=0)
    ft[l] = fp.T.astype(BF)
    gat = RingGather(cm, "y", l, lambda i, h: ft.at[i, pl.ds(h * H, H)])
    gat.run()

    lhs = jnp.concatenate([ft[i] for i in range(4)], axis=1)
    sib = {}
    for dr in (2, 3, 1, 0):
        for dx in range(4):
            at = ((r + dr) % 4) * 4 + (x + dx) % 4
            part = dot(lhs, p_v[:, pl.ds(pl.multiple_of(at * 2 * own, 2 * own), 2 * own)])
            lo, hi = part[:, :own], part[:, own:]
            mine = jnp.where(k == 0, lo, hi)
            sib_part = jnp.where(k == 0, hi, lo).astype(BF)
            for h in range(2):
                own5[h, dr, dx] = mine[h * H : (h + 1) * H]
                sb5[h, dr, dx] = sib_part[h * H : (h + 1) * H]
        sib[dr] = cm.send(sb5.at[:, dr], rb5.at[:, dr], "c")
    for dr in (2, 3, 1, 0):
        sib[dr].wait_recv()
        own5[:, dr] = own5[:, dr] + rb5[:, dr].astype(F32)
        q5[:, dr] = own5[:, dr].astype(BF)
    s0 = RingSum(cm, "z", lambda d, h: q5.at[0, d, pl.ds(2 * h, 2)], lambda i: rz0.at[i])
    s1x = RingSum(cm, "x", lambda d, h: q5.at[1, pl.ds(2 * h, 2), d], lambda i: rx1.at[i])
    s0.far()
    s1x.far()
    s0.near()
    s1x.near()
    s0.relay()
    s1x.relay()
    a0, b0 = s0.total(own5[0, 0, :2], own5[0, 0, 2:])
    a1, b1 = s1x.total(own5[1, :2, 0], own5[1, 2:, 0])
    q5[0, 0, :2] = a0.astype(BF)
    q5[0, 0, 2:] = b0.astype(BF)
    q5[1, :2, 0] = a1.astype(BF)
    q5[1, 2:, 0] = b1.astype(BF)
    hh = H // 2
    s2 = RingSum(cm, "x", lambda d, h: q5.at[0, 0, d, pl.ds(h * hh, hh)], lambda i: rx0.at[i])
    s3 = RingSum(cm, "z", lambda d, h: q5.at[1, d, 0, pl.ds(h * hh, hh)], lambda i: rz1.at[i])
    s2.far()
    s3.far()
    s2.near()
    s3.near()
    s2.relay()
    s3.relay()
    p0, p1 = s2.total(a0[0, :hh], a0[0, hh:])
    p2, p3 = s3.total(a1[0, :hh], a1[0, hh:])
    solved = jnp.concatenate([p0, p1, p2, p3], axis=0).T.astype(BF)
    solp_ref[...] = solved
    sp[l] = solved

    gat = RingGather(cm, "y", l, lambda i, h: sp.at[i, pl.ds(h * hown, hown)])
    gat.run()
    g2_v = g_v
    g2_v[...] = dot(t1t[...], sp[...].reshape(4 * own, R)).reshape(32, 8, R)
    r2_v[pl.ds(me, 1)] = g2_v[pl.ds(me, 1)]
    plane_exchange(g2_v, r2_v, 2)
    plane_wait(g2_v, r2_v, 2)
    pk[r] = dot(s1t[...], r2_v[...].reshape(256, R).astype(BF)).astype(BF)
    gat = RingGather(cm, "z", r, lambda i, h: pk.at[i, pl.ds(h * quarter, quarter)])
    gat.run()
    picked = pk[...].reshape(4 * blk, R).astype(F32).T.astype(BF)

    sib = {}
    ring = RingSum(cm, "x", lambda d, h: q7.at[d, pl.ds(h * H, H)], lambda i: rr7.at[i])
    for d in (2, 3, 1, 0):
        sb7[d] = dot(picked, b_v[:, panel_cols((x + d) % 4, 1 - k)]).astype(BF)
        sib[d] = cm.send(sb7.at[d], rb7.at[d], "c")
    for d in (2, 3, 1, 0):
        part = dot(picked, b_v[:, panel_cols((x + d) % 4, k)])
        sib[d].wait_recv()
        part = part + rb7[d].astype(F32)
        if d:
            q7[d] = part.astype(BF)
        else:
            own7[...] = part
        if d == 2:
            ring.far()
        if d == 1:
            ring.near()
    ring.relay()
    a, b = ring.total(own7[:H], own7[H:])
    ct[x, k, :H] = (yt[:H].astype(F32) - a).astype(BF)
    ct[x, k, H:] = (yt[H:].astype(F32) - b).astype(BF)

    gat = RingGather(cm, "x", x, lambda i, h: ct.at[i, k, pl.ds(h * H, H)])
    fwd = [cm.send(ct.at[x, k], ct.at[x, k], "c")]

    def pull(xx, core, first=False):
        lhs = ct[xx, core]
        rows = pl.ds(pl.multiple_of((xx * 2 + core) * n8, n8), n8)
        for d in (2, 1, 3, 0):
            cols = pl.ds(pl.multiple_of(((r + d) % 4) * n8, n8), n8)
            part = dot(lhs, a_v[rows, cols])
            acc8[d] = part if first else acc8[d] + part

    pull(x, k, True)
    gat.relay()
    gat.near()
    fwd.append(cm.send(ct.at[gat.prev, k], ct.at[gat.prev, k], "c"))
    fwd.append(cm.send(ct.at[gat.next, k], ct.at[gat.next, k], "c"))
    fwd[0].wait_recv()
    pull(x, 1 - k)
    pull(gat.prev, k)
    pull(gat.next, k)
    gat.far()
    fwd.append(cm.send(ct.at[gat.opp, k], ct.at[gat.opp, k], "c"))
    fwd[1].wait_recv()
    pull(gat.prev, 1 - k)
    fwd[2].wait_recv()
    pull(gat.next, 1 - k)
    pull(gat.opp, k)
    fwd[3].wait_recv()
    pull(gat.opp, 1 - k)
    for d in (2, 1, 3):
        q8[d] = acc8[d].astype(BF)
    ring = RingSum(cm, "z", lambda d, h: q8.at[d, pl.ds(h * H, H)], lambda i: rr8.at[i])
    ring.run()
    a, b = ring.total(acc8[0, :H], acc8[0, H:])
    out_ref[r] = jnp.concatenate([a, b], axis=0).T.astype(BF)
    gat = RingGather(cm, "z", r, lambda i, h: out_ref.at[i, pl.ds(h * half, half)])
    gat.run()
    cm.drain()


def per_device(rhs_leaf, rhs_parent, inv_leaf, panel, row_map, inv_parent):
    rows, cols = inv_leaf.shape[1:]
    pb = panel.shape[1]
    R = rhs_leaf.shape[2]
    own = rhs_parent.shape[0]
    n8, blk, H = rows // 8, pb // 4, R // 2
    prow, pcol = inv_parent.shape
    V = pltpu.VMEM
    any_spec = pl.BlockSpec(memory_space=pl.ANY)
    vmem = pl.BlockSpec(memory_space=pltpu.VMEM)
    scratch = [
        V((rows, cols), BF), V((pb, rows), BF), V((prow, pcol), BF), V((cols, R), BF), V((own, R), BF),
        V((4, n8, R), BF), V((4, n8, R), BF), V((4, n8, R), BF), V((n8, R), F32), V((6, n8 // 2, R), BF),
        V((4, 2, n8, R), BF), V((R, n8), BF),
        V((pb, R), F32), V((4, blk, R), BF), V((6, blk // 2, R), BF),
        V((32, 8, R), F32), V((32, 8, R), F32), V((32, 8, R), F32), V((32, 8, own), F32), V((32, 8, own), F32),
        V((4 * own, 256), BF), V((256, 4 * own), BF), V((256, blk), BF), V((blk, 256), BF),
        V((4, own, R), BF), V((6, own // 2, R), BF), V((2, 4, 4, 2, own, H), BF),
        V((4, own, R), BF), V((6, own // 2, R), BF), V((4, R, own), BF),
        V((2, 4, 4, H, own), BF), V((2, 4, 4, H, own), BF), V((2, 4, 4, H, own), BF), V((2, 4, 4, H, own), F32),
        V((6, 2, H, own), BF), V((6, H // 2, own), BF), V((6, 2, H, own), BF), V((6, H // 2, own), BF),
        V((4, own, R), BF), V((4, blk, R), BF),
        V((4, R, n8), BF), V((4, R, n8), BF), V((4, R, n8), BF), V((R, n8), F32), V((6, H, n8), BF),
        V((4, 2, R, n8), BF),
        V((4, R, n8), F32), V((4, R, n8), BF), V((6, H, n8), BF),
        pltpu.SemaphoreType.DMA((200,)), pltpu.SemaphoreType.DMA((200,)), pltpu.SemaphoreType.DMA((12,)),
        pltpu.SemaphoreType.DMA((3,)), pltpu.SemaphoreType.DMA((3,)),
    ]
    sol_leaf, sol_parent = pl.pallas_call(
        kernel,
        out_shape=(
            jax.ShapeDtypeStruct((4, n8, R), BF),
            jax.ShapeDtypeStruct((own, R), BF),
        ),
        in_specs=[any_spec] * 5 + [vmem],
        out_specs=(vmem, vmem),
        scratch_shapes=scratch,
        compiler_params=pltpu.CompilerParams(
            collective_id=0, has_side_effects=True, vmem_limit_bytes=60 * 1024 * 1024
        ),
    )(
        rhs_leaf[0],
        rhs_parent,
        inv_leaf[0],
        panel[0],
        inv_parent,
        row_map[0].reshape(4, blk),
    )
    return (sol_leaf.reshape(1, 4 * n8, R), sol_parent)


def solution(mesh):
    in_specs = (
        P("leaf", "col", None),
        P(("leaf", "row", "col"), None),
        P("leaf", "row", "col"),
        P("leaf", "col", "row"),
        P("leaf", "col"),
        P(("row", "col"), "leaf"),
    )
    out_specs = (P("leaf", "col", None), P(("leaf", "row", "col"), None))
    return jax.shard_map(
        per_device, mesh=mesh, in_specs=in_specs, out_specs=out_specs, check_vma=False
    )
```

time: 729 us -> 172 us (0.24)
  waiting for transfers between devices: 383 us -> 0 us
  blocking collectives: 252 us -> 0 us
  Pallas kernels: 0 us -> 164 us
  matrix products: 35.8 us -> 0 us
  local copies, waits for them, and re-layouts: 21.7 us -> 4.21 us
  other arithmetic: 15.4 us -> 0.7 us
  between operations: 13.9 us -> 0.64 us
    psum x4 -> x0, blocking collectives: 252 us -> none  [the longest x1 148 us: per_device(): reduced = lax.psum(leaf_block, ('row', 'col')).astype(jnp.bfloat16)]
    reduce_scatter x2 -> x0, waiting for transfers between devices: 235 us -> none  [the longest x1 151 us: per_device(): lax.psum_scatter(dense, 'leaf', scatter_dimension=0, tiled=True)]
    pallas_call x0 -> x1, Pallas kernels: none -> 164 us  [per_device(): pl.pallas_call(kernel, out_shape=(jax.ShapeDtypeStruct((4, n8, R), BF), j...]
    all_gather x1 -> x0, waiting for transfers between devices: 82.3 us -> none  [per_device(): lax.all_gather(sol_parent, ('leaf', 'row', 'col'), axis=0, tiled=True)]
    psum x1 -> x0, waiting for transfers between devices: 65.8 us -> none  [per_device(): coupling = lax.psum(coupling_part, 'col')]
    dot_general x6 -> x0, matrix products: 35.8 us -> none  [the longest x1 8.46 us: per_device(): lax.dot_general(inv_leaf[0], corrected, (((0,), (0,)), ((), ())), preferr...]
    scatter-add x1 -> x0, other arithmetic: 12.3 us -> none  [dense_updates(): dense = dense.at[row_map[0]].add(-update)]
    all_gather x1 -> x0, local copies, waits for them, and re-layouts: 11.9 us -> none  [per_device(): lax.all_gather(sol_parent, ('leaf', 'row', 'col'), axis=0, tiled=True)]
  transfers between devices with their start and end apart: 4 -> 0, of which waited for: 4 -> 0; matrix products, arithmetic and copies ran while one was open for 0% -> 0% of each run, Pallas kernels for 0% -> 0%
where the time goes in v1:
time: 172 us; the launch traced here: 169 us
  Pallas kernels  164 us (95%)
  local copies, waits for them, and re-layouts  4.21 us (2%)
    pallas_call x1, Pallas kernels, per_device(): pl.pallas_call(kernel, out_shape=(jax.ShapeDtypeStruct((4, n8, R), BF), j...  164 us
    unnamed x2, local copies, waits for them, and re-layouts  3.54 us

profile of v1, /device:TPU:1, one launch (start us, length us, event | category | flops | bytes accessed | tf_op | source)
XLA Modules:
  0.0 169.1 jit_solution(5252574270709932498)
XLA Ops:
  0.6 0.7 reduce
  1.3 0.7 reshape_squeeze.3.rm_ref
  2.0 163.6 %shard_map.77 = (bf16[4,384,256]{2,1,0:T(8,128)(2,1)}, bf16[128,256]{1,0:T(8,128)(2,1)}) custom-call(bf16[1536,256]{1,0:T(8,128)(2,1)} %bitcast.7, bf16[128,256]{1,0:T(8,128)(2,1)} %rp_hbm.1, bf16[3072,1536]{1,0:T(8,128)(2,1)} %bitcast.4, bf16[768,3072]{1,0:T(8,128)(2,1)} %bitcast.5, bf16[512,4096]{1,0:T(8,128)(2,1)} %p_hbm.1, s32[4,192]{1,0:T(4,128)} %reshape_squeeze.3.rm_ref), custom_call_target="tpu_custom_call" | custom-call | tf_op jit(solution)/shard_map/pallas_call | solution.py:520
  165.6 2.1 %copy.10 = bf16[1,1536,256]{2,1,0:T(8,128)(2,1)} copy(bf16[1,1536,256]{2,1,0:T(8,128)(2,1)} %bitcast.6) | data formatting | bytes 1572864
  167.7 1.5 copy.11

commit v2 on v0

v2 whole, which is shorter than its diff:
```python
import jax
import jax.numpy as jnp
from jax import lax
from jax.experimental import pallas as pl
from jax.experimental.pallas import tpu as pltpu
from jax.sharding import PartitionSpec as P

MESH = pl.DeviceIdType.MESH
BF = jnp.bfloat16
F32 = jnp.float32


def dot(a, b):
    return jnp.dot(a, b, preferred_element_type=F32)


class Comm:
    def __init__(self, ssem, rsem):
        self.ssem, self.rsem, self.n, self.sent = ssem, rsem, 0, []
        self.l, self.r, self.c = (lax.axis_index(a) for a in ("leaf", "row", "col"))
        self.x, self.k = self.c // 2, self.c % 2

    def at(self, axis, delta):
        if axis == "x":
            return (self.l, self.r, ((self.x + delta + 4) % 4) * 2 + self.k)
        if axis == "z":
            return (self.l, (self.r + delta + 4) % 4, self.c)
        if axis == "y":
            return ((self.l + delta + 4) % 4, self.r, self.c)
        return (self.l, self.r, self.x * 2 + 1 - self.k)

    def make(self, src, dst, device):
        at = self.n
        self.n += 1
        return pltpu.make_async_remote_copy(
            src_ref=src,
            dst_ref=dst,
            send_sem=self.ssem.at[at],
            recv_sem=self.rsem.at[at],
            device_id=device,
            device_id_type=MESH,
        )

    def send(self, src, dst, axis, delta=0):
        copy = self.make(src, dst, self.at(axis, delta))
        copy.start()
        self.sent.append(copy)
        return copy

    def drain(self):
        for copy in self.sent:
            copy.wait_send()
        self.sent = []


class Sum:
    def __init__(self, comm, axis, q, slot):
        self.comm, self.axis, self.q, self.slot, self.copies = comm, axis, q, slot, {}

    def put(self, d):
        self.copies[d] = self.comm.send(self.q(d), self.slot(d - 1), self.axis, d)

    def run(self):
        for d in (2, 1, 3):
            self.put(d)

    def total(self, own):
        for d in (1, 3, 2):
            self.copies[d].wait_recv()
            own = own + self.slot(d - 1)[...].astype(F32)
        return own


class Gather:
    def __init__(self, comm, axis, me, g):
        self.me = me
        self.copies = {d: comm.send(g(me), g(me), axis, d) for d in (2, 1, 3)}

    def wait(self, d):
        self.copies[d].wait_recv()
        return (self.me + 4 - d) % 4

    def run(self):
        for d in (1, 3, 2):
            self.wait(d)


def kernel(
    x_hbm, rp_hbm, a_hbm, b_hbm, p_hbm, rm_ref,
    out_ref, solp_ref,
    a_v, b_v, p_v, x_v, rp_v,
    sb1, rb1, q1, own1, rr1, y_v, yt,
    u_acc, g32, g_v, r1_v, r2_v, qs, qr, t1, t1t, s1, s1t,
    q3, rr3, gred, q4, rr4, ft,
    sb5, rb5, q5, own5, rz0, rx0, rx1, rz1,
    sp, sb7, rb7, q7, own7, rr7, ct,
    acc8, q8, rr8,
    ssem, rsem, lsem, asem, bsem,
):
    cm = Comm(ssem, rsem)
    l, r, c, x, k = cm.l, cm.r, cm.c, cm.x, cm.k
    me = r * 8 + c
    n8 = y_v.shape[2]
    R = x_v.shape[1]
    H = R // 2
    own = rp_v.shape[0]
    blk = s1t.shape[1]

    loads = [pltpu.make_async_copy(x_hbm, x_v, lsem.at[0])]
    for i, d in enumerate((2, 3, 1, 0)):
        for j, core in enumerate((1 - k, k)):
            rows = pl.ds(pl.multiple_of((((x + d) % 4) * 2 + core) * n8, n8), n8)
            loads.append(pltpu.make_async_copy(a_hbm.at[rows], a_v.at[rows], lsem.at[1 + 2 * i + j]))
    loads.append(pltpu.make_async_copy(rp_hbm, rp_v, lsem.at[9]))
    loads.append(pltpu.make_async_copy(b_hbm, b_v, lsem.at[10]))
    loads.append(pltpu.make_async_copy(p_hbm, p_v, lsem.at[11]))
    for load in loads:
        load.start()

    barrier = pltpu.get_barrier_semaphore()

    def greet(n, _):
        to = (me + n) % 32
        pl.semaphore_signal(barrier, inc=1, device_id=(l, to // 8, to % 8), device_id_type=MESH)
        return 0

    lax.fori_loop(1, 32, greet, 0)
    for d in (1, 2, 3):
        pl.semaphore_signal(barrier, inc=1, device_id=((l + d) % 4, r, c), device_id_type=MESH)

    def a_rows(d, core):
        return pl.ds(pl.multiple_of((((x + d) % 4) * 2 + core) * n8, n8), n8)

    sib = {}
    loads[0].wait()
    xv = x_v[...]
    ring = Sum(cm, "x", lambda d: q1.at[d], lambda i: rr1.at[i])
    for i, d in enumerate((2, 3, 1, 0)):
        loads[1 + 2 * i].wait()
        sb1[d] = dot(a_v[a_rows(d, 1 - k), :], xv).astype(BF)
        if i == 0:
            pl.semaphore_wait(barrier, 34)
        sib[d] = cm.send(sb1.at[d], rb1.at[d], "c")
    for i, d in enumerate((2, 3, 1, 0)):
        loads[2 + 2 * i].wait()
        part = dot(a_v[a_rows(d, k), :], xv)
        sib[d].wait_recv()
        part = part + rb1[d].astype(F32)
        if d:
            q1[d] = part.astype(BF)
            ring.put(d)
        else:
            own1[...] = part

    shift = own.bit_length() - 1
    before = lax.broadcasted_iota(jnp.int32, (blk, blk), 0) < lax.broadcasted_iota(jnp.int32, (blk, blk), 1)
    for i in range(4):
        e = rm_ref[i : i + 1, :]
        owner = lax.shift_right_logical(e, shift)
        local = lax.bitwise_and(e, own - 1).astype(F32)
        across = jnp.broadcast_to(owner.astype(F32), (blk, blk))
        rank = jnp.sum(jnp.where((across == across.T) & before, 1.0, 0.0), axis=0, keepdims=True)
        place = lax.bitwise_and(owner, 31) * 8 + lax.shift_right_logical(owner, 5) * 2
        place = place.astype(F32) + rank
        pick = jnp.where(
            lax.broadcasted_iota(jnp.int32, (256, blk), 0).astype(F32) == jnp.broadcast_to(place, (256, blk)), 1.0, 0.0
        )
        s1[i] = pick.astype(BF)
        near = (lax.broadcasted_iota(jnp.int32, (64, blk), 0) + r * 64).astype(F32)
        where = jnp.where(near == jnp.broadcast_to(place, (64, blk)), jnp.broadcast_to(local + 1.0, (64, blk)), 0.0)
        qv = jnp.sum(where, axis=1, keepdims=True)
        qs[:, i * 8 : (i + 1) * 8, :] = jnp.broadcast_to(qv, (64, own)).reshape(8, 8, own)
    qr[pl.ds(c, 1)] = qs[pl.ds(c, 1)]

    def row_copy(n):
        to = (c + n) % 8
        return pltpu.make_async_remote_copy(
            src_ref=qs.at[to], dst_ref=qr.at[c], send_sem=asem.at[0], recv_sem=bsem.at[0],
            device_id=(l, r, to), device_id_type=MESH,
        )

    for n in range(1, 8):
        row_copy(n).start()

    tot = ring.total(own1[...])
    y_v[x, k] = tot.astype(BF)

    gat = Gather(cm, "x", x, lambda i: y_v.at[i, k])
    fwd = {0: cm.send(y_v.at[x, k], y_v.at[x, k], "c")}
    yt[...] = tot.T.astype(BF)
    loads[10].wait()

    def panel_cols(xx, core):
        return pl.ds(pl.multiple_of((xx * 2 + core) * n8, n8), n8)

    def push(xx, core, first=False):
        part = dot(b_v[:, panel_cols(xx, core)], y_v[xx, core])
        u_acc[...] = part if first else u_acc[...] + part

    push(x, k, True)
    fwd[0].wait_recv()
    push(x, 1 - k)
    at = {}
    for d in (1, 3, 2):
        at[d] = gat.wait(d)
        fwd[d] = cm.send(y_v.at[at[d], k], y_v.at[at[d], k], "c")
        push(at[d], k)
        if d != 1:
            last = 1 if d == 3 else 3
            fwd[last].wait_recv()
            push(at[last], 1 - k)
    fwd[2].wait_recv()
    push(at[2], 1 - k)

    def plane_exchange(src, src_at, dst, which):
        def one(n, _):
            to = (me + n) % 32
            pltpu.make_async_remote_copy(
                src_ref=src.at[src_at(to)], dst_ref=dst.at[me], send_sem=asem.at[which], recv_sem=bsem.at[which],
                device_id=(l, to // 8, to % 8), device_id_type=MESH,
            ).start()
            return 0

        lax.fori_loop(1, 32, one, 0)

    def plane_wait(dst, which):
        copy = pltpu.make_async_remote_copy(
            src_ref=dst.at[pl.ds(0, 31)], dst_ref=dst.at[pl.ds(0, 31)], send_sem=asem.at[which],
            recv_sem=bsem.at[which], device_id=cm.at("c", 0), device_id_type=MESH,
        )
        copy.wait_send()
        copy.wait_recv()

    for i in range(4):
        rows = u_acc[i * blk : (i + 1) * blk].astype(BF)
        g32[:, i * 8 : (i + 1) * 8, :] = dot(s1[i], rows).reshape(32, 8, R)
    g_v[...] = g32[...].astype(BF)
    plane_exchange(g_v, lambda to: to, r1_v, 1)
    r1_v[pl.ds(me, 1)] = g_v[pl.ds(me, 1)]

    copy = pltpu.make_async_remote_copy(
        src_ref=qs.at[pl.ds(0, 7)], dst_ref=qr.at[pl.ds(0, 7)], send_sem=asem.at[0], recv_sem=bsem.at[0],
        device_id=cm.at("c", 0), device_id_type=MESH,
    )
    copy.wait_send()
    copy.wait_recv()
    seen = qr[...].reshape(256, own)
    lane = lax.broadcasted_iota(jnp.int32, (256, own), 1).astype(F32) + 1.0
    leaf_of = lax.bitwise_and(
        lax.shift_right_logical(lax.broadcasted_iota(jnp.int32, (256, own), 0), 1), 3
    )
    for i in range(4):
        table = jnp.where((seen == lane) & (leaf_of == i), 1.0, 0.0)
        t1t[:, i * own : (i + 1) * own] = table.astype(BF)
        t1[i * own : (i + 1) * own, :] = table.T.astype(BF)

    plane_wait(r1_v, 1)
    got = r1_v[0:8].astype(F32)
    for i in range(1, 4):
        got = got + r1_v[8 * i : 8 * i + 8].astype(F32)
    got = got.reshape(256, R).astype(BF)

    def t_rows(d):
        return t1[pl.ds(pl.multiple_of(((l + d) % 4) * own, own), own), :]

    ring = Sum(cm, "y", lambda d: q3.at[d], lambda i: rr3.at[i])
    for d in (2, 1, 3):
        q3[d] = dot(t_rows(d), got).astype(BF)
        ring.put(d)
    tot = dot(t_rows(0), got)
    loads[9].wait()
    tot = rp_v[...].astype(F32) - ring.total(tot)
    for h in range(2):
        gred[h, r, x, k] = tot[:, h * H : (h + 1) * H].astype(BF)

    g0 = Gather(cm, "x", x, lambda i: gred.at[0, r, i, k])
    g1 = Gather(cm, "z", r, lambda i: gred.at[1, i, x, k])
    for i in range(4):
        s1t[i] = s1[i].astype(F32).T.astype(BF)
    g0.run()
    g2 = Gather(cm, "z", r, lambda i: gred.at[0, i, :, k])
    g1.run()
    g3 = Gather(cm, "x", x, lambda i: gred.at[1, :, i, k])
    fwd = [cm.send(gred.at[0, r, :, k], gred.at[0, r, :, k], "c")]
    fwd.append(cm.send(gred.at[1, :, x, k], gred.at[1, :, x, k], "c"))
    loads[11].wait()
    for d in (1, 3, 2):
        i = g2.wait(d)
        fwd.append(cm.send(gred.at[0, i, :, k], gred.at[0, i, :, k], "c"))
        i = g3.wait(d)
        fwd.append(cm.send(gred.at[1, :, i, k], gred.at[1, :, i, k], "c"))
    for copy in fwd:
        copy.wait_recv()

    parent = None
    for i in range(4):
        rhs = jnp.concatenate([gred[h, i].reshape(8 * own, H) for h in range(2)], axis=1)
        part = dot(p_v[:, i * 8 * own : (i + 1) * 8 * own], rhs)
        parent = part if parent is None else parent + part
    u_acc[: 4 * own] = parent

    def f_rows(d):
        return u_acc[pl.ds(pl.multiple_of(((l + d) % 4) * own, own), own), :]

    ring = Sum(cm, "y", lambda d: q4.at[d], lambda i: rr4.at[i])
    for d in (2, 1, 3):
        q4[d] = f_rows(d).astype(BF)
        ring.put(d)
    ft[l] = ring.total(f_rows(0)).T.astype(BF)
    Gather(cm, "y", l, lambda i: ft.at[i]).run()

    lhs = jnp.concatenate([ft[i] for i in range(4)], axis=1)
    sib = {}
    for dr in (2, 3, 1, 0):
        for dx in range(4):
            block = ((r + dr) % 4) * 4 + (x + dx) % 4
            part = dot(lhs, p_v[:, pl.ds(pl.multiple_of(block * 2 * own, 2 * own), 2 * own)])
            lo, hi = part[:, :own], part[:, own:]
            mine = jnp.where(k == 0, lo, hi)
            sib_part = jnp.where(k == 0, hi, lo).astype(BF)
            for h in range(2):
                own5[h, dr, dx] = mine[h * H : (h + 1) * H]
                sb5[h, dr, dx] = sib_part[h * H : (h + 1) * H]
        sib[dr] = cm.send(sb5.at[:, dr], rb5.at[:, dr], "c")
    z0 = Sum(cm, "z", lambda d: q5.at[0, d], lambda i: rz0.at[i])
    x1 = Sum(cm, "x", lambda d: q5.at[1, :, d], lambda i: rx1.at[i])
    for dr in (2, 3, 1, 0):
        sib[dr].wait_recv()
        own5[:, dr] = own5[:, dr] + rb5[:, dr].astype(F32)
        q5[:, dr] = own5[:, dr].astype(BF)
        if dr:
            z0.put(dr)
    x1.run()
    tot0 = z0.total(own5[0, 0])
    q5[0, 0] = tot0.astype(BF)
    x0 = Sum(cm, "x", lambda d: q5.at[0, 0, d], lambda i: rx0.at[i])
    x0.run()
    tot1 = x1.total(own5[1, :, 0])
    q5[1, :, 0] = tot1.astype(BF)
    z1 = Sum(cm, "z", lambda d: q5.at[1, d, 0], lambda i: rz1.at[i])
    z1.run()
    lo = x0.total(tot0[0])
    hi = z1.total(tot1[0])
    solved = jnp.concatenate([lo, hi], axis=0).T.astype(BF)
    sp[l] = solved

    gat = Gather(cm, "y", l, lambda i: sp.at[i])
    solp_ref[...] = solved
    gat.run()
    g8 = dot(t1t[...], sp[...].reshape(4 * own, R)).astype(BF).reshape(8, 32, R)
    g_v[0:8] = g8
    plane_exchange(g_v, lambda to: to % 8, r2_v, 2)
    r2_v[pl.ds(me, 1)] = g_v[pl.ds(c, 1)]
    plane_wait(r2_v, 2)
    g32[...] = r2_v[...].astype(F32)
    picked = jnp.concatenate(
        [dot(s1t[i], g32[:, i * 8 : (i + 1) * 8, :].reshape(256, R).astype(BF)) for i in range(4)], axis=0
    )
    picked = picked.T.astype(BF)

    sib = {}
    ring = Sum(cm, "x", lambda d: q7.at[d], lambda i: rr7.at[i])
    for d in (2, 3, 1, 0):
        sb7[d] = dot(picked, b_v[:, panel_cols((x + d) % 4, 1 - k)]).astype(BF)
        sib[d] = cm.send(sb7.at[d], rb7.at[d], "c")
    for d in (2, 3, 1, 0):
        part = dot(picked, b_v[:, panel_cols((x + d) % 4, k)])
        sib[d].wait_recv()
        part = part + rb7[d].astype(F32)
        if d:
            q7[d] = part.astype(BF)
            ring.put(d)
        else:
            own7[...] = part
    tot = ring.total(own7[...])
    ct[x, k] = (yt[...].astype(F32) - tot).astype(BF)

    gat = Gather(cm, "x", x, lambda i: ct.at[i, k])
    fwd = {0: cm.send(ct.at[x, k], ct.at[x, k], "c")}
    ring = Sum(cm, "z", lambda d: q8.at[d], lambda i: rr8.at[i])

    def pull(xx, core, first=False, last=False):
        lhs = ct[xx, core]
        rows = pl.ds(pl.multiple_of((xx * 2 + core) * n8, n8), n8)
        for d in (2, 1, 3, 0):
            cols = pl.ds(pl.multiple_of(((r + d) % 4) * n8, n8), n8)
            part = dot(lhs, a_v[rows, cols])
            part = part if first else acc8[d] + part
            if last and d:
                q8[d] = part.astype(BF)
                ring.put(d)
            else:
                acc8[d] = part

    pull(x, k, True)
    fwd[0].wait_recv()
    pull(x, 1 - k)
    at = {}
    for d in (1, 3, 2):
        at[d] = gat.wait(d)
        fwd[d] = cm.send(ct.at[at[d], k], ct.at[at[d], k], "c")
        pull(at[d], k)
        if d != 1:
            last = 1 if d == 3 else 3
            fwd[last].wait_recv()
            pull(at[last], 1 - k)
    fwd[2].wait_recv()
    pull(at[2], 1 - k, last=True)
    out_ref[r] = ring.total(acc8[0]).T.astype(BF)
    Gather(cm, "z", r, lambda i: out_ref.at[i]).run()
    cm.drain()


def per_device(rhs_leaf, rhs_parent, inv_leaf, panel, row_map, inv_parent):
    rows, cols = inv_leaf.shape[1:]
    pb = panel.shape[1]
    R = rhs_leaf.shape[2]
    own = rhs_parent.shape[0]
    n8, blk, H = rows // 8, pb // 4, R // 2
    prow, pcol = inv_parent.shape
    V = pltpu.VMEM
    any_spec = pl.BlockSpec(memory_space=pl.ANY)
    vmem = pl.BlockSpec(memory_space=pltpu.VMEM)
    scratch = [
        V((rows, cols), BF), V((pb, rows), BF), V((prow, pcol), BF), V((cols, R), BF), V((own, R), BF),
        V((4, n8, R), BF), V((4, n8, R), BF), V((4, n8, R), BF), V((n8, R), F32), V((3, n8, R), BF),
        V((4, 2, n8, R), BF), V((R, n8), BF),
        V((pb, R), F32), V((32, 32, R), F32), V((32, 32, R), BF), V((32, 32, R), BF), V((32, 32, R), BF),
        V((8, 32, own), F32), V((8, 32, own), F32),
        V((4 * own, 256), BF), V((256, 4 * own), BF), V((4, 256, blk), BF), V((4, blk, 256), BF),
        V((4, own, R), BF), V((3, own, R), BF), V((2, 4, 4, 2, own, H), BF),
        V((4, own, R), BF), V((3, own, R), BF), V((4, R, own), BF),
        V((2, 4, 4, H, own), BF), V((2, 4, 4, H, own), BF), V((2, 4, 4, H, own), BF), V((2, 4, 4, H, own), F32),
        V((3, 4, H, own), BF), V((3, H, own), BF), V((3, 4, H, own), BF), V((3, H, own), BF),
        V((4, own, R), BF),
        V((4, R, n8), BF), V((4, R, n8), BF), V((4, R, n8), BF), V((R, n8), F32), V((3, R, n8), BF),
        V((4, 2, R, n8), BF),
        V((4, R, n8), F32), V((4, R, n8), BF), V((3, R, n8), BF),
        pltpu.SemaphoreType.DMA((100,)), pltpu.SemaphoreType.DMA((100,)), pltpu.SemaphoreType.DMA((12,)),
        pltpu.SemaphoreType.DMA((3,)), pltpu.SemaphoreType.DMA((3,)),
    ]
    sol_leaf, sol_parent = pl.pallas_call(
        kernel,
        out_shape=(
            jax.ShapeDtypeStruct((4, n8, R), BF),
            jax.ShapeDtypeStruct((own, R), BF),
        ),
        in_specs=[any_spec] * 5 + [vmem],
        out_specs=(vmem, vmem),
        scratch_shapes=scratch,
        compiler_params=pltpu.CompilerParams(
            collective_id=0, has_side_effects=True, vmem_limit_bytes=60 * 1024 * 1024
        ),
    )(
        rhs_leaf[0],
        rhs_parent,
        inv_leaf[0],
        panel[0],
        inv_parent,
        row_map[0].reshape(4, blk),
    )
    return (sol_leaf.reshape(1, 4 * n8, R), sol_parent)


def solution(mesh):
    in_specs = (
        P("leaf", "col", None),
        P(("leaf", "row", "col"), None),
        P("leaf", "row", "col"),
        P("leaf", "col", "row"),
        P("leaf", "col"),
        P(("row", "col"), "leaf"),
    )
    out_specs = (P("leaf", "col", None), P(("leaf", "row", "col"), None))
    return jax.shard_map(
        per_device, mesh=mesh, in_specs=in_specs, out_specs=out_specs, check_vma=False
    )
```

time: 729 us -> 165 us (0.23)
  waiting for transfers between devices: 383 us -> 0 us
  blocking collectives: 252 us -> 0 us
  Pallas kernels: 0 us -> 159 us
  matrix products: 35.8 us -> 0 us
  local copies, waits for them, and re-layouts: 21.7 us -> 4.21 us
  other arithmetic: 15.4 us -> 0.7 us
  between operations: 13.9 us -> 0.64 us
    psum x4 -> x0, blocking collectives: 252 us -> none  [the longest x1 148 us: per_device(): reduced = lax.psum(leaf_block, ('row', 'col')).astype(jnp.bfloat16)]
    reduce_scatter x2 -> x0, waiting for transfers between devices: 235 us -> none  [the longest x1 151 us: per_device(): lax.psum_scatter(dense, 'leaf', scatter_dimension=0, tiled=True)]
    pallas_call x0 -> x1, Pallas kernels: none -> 159 us  [per_device(): pl.pallas_call(kernel, out_shape=(jax.ShapeDtypeStruct((4, n8, R), BF), j...]
    all_gather x1 -> x0, waiting for transfers between devices: 82.3 us -> none  [per_device(): lax.all_gather(sol_parent, ('leaf', 'row', 'col'), axis=0, tiled=True)]
    psum x1 -> x0, waiting for transfers between devices: 65.8 us -> none  [per_device(): coupling = lax.psum(coupling_part, 'col')]
    dot_general x6 -> x0, matrix products: 35.8 us -> none  [the longest x1 8.46 us: per_device(): lax.dot_general(inv_leaf[0], corrected, (((0,), (0,)), ((), ())), preferr...]
    scatter-add x1 -> x0, other arithmetic: 12.3 us -> none  [dense_updates(): dense = dense.at[row_map[0]].add(-update)]
    all_gather x1 -> x0, local copies, waits for them, and re-layouts: 11.9 us -> none  [per_device(): lax.all_gather(sol_parent, ('leaf', 'row', 'col'), axis=0, tiled=True)]
  transfers between devices with their start and end apart: 4 -> 0, of which waited for: 4 -> 0; matrix products, arithmetic and copies ran while one was open for 0% -> 0% of each run, Pallas kernels for 0% -> 0%
where the time goes in v2:
time: 165 us
  Pallas kernels  159 us (96%)
  local copies, waits for them, and re-layouts  4.21 us (3%)
    pallas_call x1, Pallas kernels, per_device(): pl.pallas_call(kernel, out_shape=(jax.ShapeDtypeStruct((4, n8, R), BF), j...  159 us
    unnamed x2, local copies, waits for them, and re-layouts  3.54 us

profile of v2, /device:TPU:1, one launch (start us, length us, event | category | flops | bytes accessed | tf_op | source)
XLA Modules:
  0.0 165.0 jit_solution(561038240655182303)
XLA Ops:
  0.6 0.7 reduce
  1.3 0.7 reshape_squeeze.3.rm_ref
  2.0 159.4 %shard_map.77 = (bf16[4,384,256]{2,1,0:T(8,128)(2,1)}, bf16[128,256]{1,0:T(8,128)(2,1)}) custom-call(bf16[1536,256]{1,0:T(8,128)(2,1)} %bitcast.7, bf16[128,256]{1,0:T(8,128)(2,1)} %rp_hbm.1, bf16[3072,1536]{1,0:T(8,128)(2,1)} %bitcast.4, bf16[768,3072]{1,0:T(8,128)(2,1)} %bitcast.5, bf16[512,4096]{1,0:T(8,128)(2,1)} %p_hbm.1, s32[4,192]{1,0:T(4,128)} %reshape_squeeze.3.rm_ref), custom_call_target="tpu_custom_call" | custom-call | tf_op jit(solution)/shard_map/pallas_call | solution.py:442
  161.5 2.1 %copy.10 = bf16[1,1536,256]{2,1,0:T(8,128)(2,1)} copy(bf16[1,1536,256]{2,1,0:T(8,128)(2,1)} %bitcast.6) | data formatting | bytes 1572864
  163.5 1.5 copy.11

commit v3 on v0

v3 whole, which is shorter than its diff:
```python
import jax
import jax.numpy as jnp
from jax import lax
from jax.experimental import pallas as pl
from jax.experimental.pallas import tpu as pltpu
from jax.sharding import PartitionSpec as P

MESH = pl.DeviceIdType.MESH
BF = jnp.bfloat16
F32 = jnp.float32


def dot(a, b):
    return jnp.dot(a, b, preferred_element_type=F32)


class Comm:
    def __init__(self, ssem, rsem):
        self.ssem, self.rsem, self.n, self.sent = ssem, rsem, 0, []
        self.l, self.r, self.c = (lax.axis_index(a) for a in ("leaf", "row", "col"))
        self.x, self.k = self.c // 2, self.c % 2

    def at(self, axis, delta):
        if axis == "x":
            return (self.l, self.r, ((self.x + delta + 4) % 4) * 2 + self.k)
        if axis == "z":
            return (self.l, (self.r + delta + 4) % 4, self.c)
        if axis == "y":
            return ((self.l + delta + 4) % 4, self.r, self.c)
        return (self.l, self.r, self.x * 2 + 1 - self.k)

    def make(self, src, dst, device):
        at = self.n
        self.n += 1
        return pltpu.make_async_remote_copy(
            src_ref=src,
            dst_ref=dst,
            send_sem=self.ssem.at[at],
            recv_sem=self.rsem.at[at],
            device_id=device,
            device_id_type=MESH,
        )

    def send(self, src, dst, axis, delta=0):
        copy = self.make(src, dst, self.at(axis, delta))
        copy.start()
        self.sent.append(copy)
        return copy

    def drain(self):
        for copy in self.sent:
            copy.wait_send()
        self.sent = []


class Sum:
    def __init__(self, comm, axis, q, slot):
        self.comm, self.axis, self.q, self.slot, self.copies = comm, axis, q, slot, {}

    def put(self, d):
        self.copies[d] = self.comm.send(self.q(d), self.slot(d - 1), self.axis, d)

    def run(self):
        for d in (2, 1, 3):
            self.put(d)

    def total(self, own):
        for d in (1, 3, 2):
            self.copies[d].wait_recv()
            own = own + self.slot(d - 1)[...].astype(F32)
        return own


class Gather:
    def __init__(self, comm, axis, me, g):
        self.me = me
        self.copies = {d: comm.send(g(me), g(me), axis, d) for d in (2, 1, 3)}

    def wait(self, d):
        self.copies[d].wait_recv()
        return (self.me + 4 - d) % 4

    def run(self):
        for d in (1, 3, 2):
            self.wait(d)


def kernel(
    x_hbm, rp_hbm, a_hbm, b_hbm, p_hbm, rm_ref,
    out_ref, solp_ref,
    a_v, b_v, p_v, x_v, rp_v,
    sb1_, rb1_, q1_, own1_, rr1_, y_, yt_,
    u_acc_, g32_, g_, r1_, r2_, qs, qr, t1, t1t, s1, s1t,
    q3_, rr3_, gred_, q4_, rr4_, ft_,
    sb5_, rb5_, q5_, own5_, ra5_, rb5b_,
    sp_, sb7_, rb7_, q7_, own7_, rr7_, ct_,
    acc8_, q8_, rr8_,
    ssem, rsem, lsem, asem, bsem,
):
    cm = Comm(ssem, rsem)
    l, r, c, x, k = cm.l, cm.r, cm.c, cm.x, cm.k
    me = r * 8 + c
    n8 = y_.shape[3]
    W = x_v.shape[1] // 2
    own = rp_v.shape[0]
    blk = s1t.shape[1]
    order = ((1, 2), (1, 3), (0, 2), (1, 1), (0, 3), (1, 0), (0, 1), (0, 0))

    def a_rows(d, away):
        core = 1 - k if away else k
        return pl.ds(pl.multiple_of((((x + d) % 4) * 2 + core) * n8, n8), n8)

    loads = [pltpu.make_async_copy(x_hbm, x_v, lsem.at[0])]
    for i, (away, d) in enumerate(order):
        rows = a_rows(d, away)
        loads.append(pltpu.make_async_copy(a_hbm.at[rows], a_v.at[rows], lsem.at[1 + i]))
    loads.append(pltpu.make_async_copy(rp_hbm, rp_v, lsem.at[9]))
    loads.append(pltpu.make_async_copy(b_hbm, b_v, lsem.at[10]))
    loads.append(pltpu.make_async_copy(p_hbm, p_v, lsem.at[11]))
    for load in loads:
        load.start()
    loaded = set()

    def need(i):
        if i not in loaded:
            loaded.add(i)
            loads[i].wait()

    barrier = pltpu.get_barrier_semaphore()

    def greet(n, _):
        to = (me + n) % 32
        pl.semaphore_signal(barrier, inc=1, device_id=(l, to // 8, to % 8), device_id_type=MESH)
        return 0

    lax.fori_loop(1, 32, greet, 0)
    for d in (1, 2, 3):
        pl.semaphore_signal(barrier, inc=1, device_id=((l + d) % 4, r, c), device_id_type=MESH)

    def panel_cols(xx, core):
        return pl.ds(pl.multiple_of((xx * 2 + core) * n8, n8), n8)

    def row_wait():
        copy = pltpu.make_async_remote_copy(
            src_ref=qs.at[pl.ds(0, 7)], dst_ref=qr.at[pl.ds(0, 7)], send_sem=asem.at[0], recv_sem=bsem.at[0],
            device_id=cm.at("c", 0), device_id_type=MESH,
        )
        copy.wait_send()
        copy.wait_recv()

    def plane_exchange(src, src_at, dst, which):
        def one(n, _):
            to = (me + n) % 32
            pltpu.make_async_remote_copy(
                src_ref=src.at[src_at(to)], dst_ref=dst.at[me], send_sem=asem.at[which], recv_sem=bsem.at[which],
                device_id=(l, to // 8, to % 8), device_id_type=MESH,
            ).start()
            return 0

        lax.fori_loop(1, 32, one, 0)

    def plane_wait(dst, which):
        copy = pltpu.make_async_remote_copy(
            src_ref=dst.at[pl.ds(0, 31)], dst_ref=dst.at[pl.ds(0, 31)], send_sem=asem.at[which],
            recv_sem=bsem.at[which], device_id=cm.at("c", 0), device_id_type=MESH,
        )
        copy.wait_send()
        copy.wait_recv()

    def slot_tables():
        shift = own.bit_length() - 1
        before = lax.broadcasted_iota(jnp.int32, (blk, blk), 0) < lax.broadcasted_iota(jnp.int32, (blk, blk), 1)
        for i in range(4):
            e = rm_ref[i : i + 1, :]
            owner = lax.shift_right_logical(e, shift)
            local = lax.bitwise_and(e, own - 1).astype(F32)
            across = jnp.broadcast_to(owner.astype(F32), (blk, blk))
            rank = jnp.sum(jnp.where((across == across.T) & before, 1.0, 0.0), axis=0, keepdims=True)
            place = lax.bitwise_and(owner, 31) * 8 + lax.shift_right_logical(owner, 5) * 2
            place = place.astype(F32) + rank
            pick = jnp.where(
                lax.broadcasted_iota(jnp.int32, (256, blk), 0).astype(F32) == jnp.broadcast_to(place, (256, blk)),
                1.0,
                0.0,
            )
            s1[i] = pick.astype(BF)
            near = (lax.broadcasted_iota(jnp.int32, (64, blk), 0) + r * 64).astype(F32)
            where = jnp.where(near == jnp.broadcast_to(place, (64, blk)), jnp.broadcast_to(local + 1.0, (64, blk)), 0.0)
            qv = jnp.sum(where, axis=1, keepdims=True)
            qs[:, i * 8 : (i + 1) * 8, :] = jnp.broadcast_to(qv, (64, own)).reshape(8, 8, own)
        qr[pl.ds(c, 1)] = qs[pl.ds(c, 1)]
        for n in range(1, 8):
            to = (c + n) % 8
            pltpu.make_async_remote_copy(
                src_ref=qs.at[to], dst_ref=qr.at[c], send_sem=asem.at[0], recv_sem=bsem.at[0],
                device_id=(l, r, to), device_id_type=MESH,
            ).start()

    def parent_tables():
        row_wait()
        seen = qr[...].reshape(256, own)
        lane = lax.broadcasted_iota(jnp.int32, (256, own), 1).astype(F32) + 1.0
        leaf_of = lax.bitwise_and(
            lax.shift_right_logical(lax.broadcasted_iota(jnp.int32, (256, own), 0), 1), 3
        )
        for i in range(4):
            table = jnp.where((seen == lane) & (leaf_of == i), 1.0, 0.0)
            t1t[:, i * own : (i + 1) * own] = table.astype(BF)
            t1[i * own : (i + 1) * own, :] = table.T.astype(BF)

    def chain(hf):
        sb1, rb1, q1, own1, rr1, y_v, yt = (v.at[hf] for v in (sb1_, rb1_, q1_, own1_, rr1_, y_, yt_))
        u_acc, g32, g_v, r1_v, r2_v = (v.at[hf] for v in (u_acc_, g32_, g_, r1_, r2_))
        q3, rr3, gred, q4, rr4, ft = (v.at[hf] for v in (q3_, rr3_, gred_, q4_, rr4_, ft_))
        sb5, rb5, q5, own5, ra5, rb5b = (v.at[hf] for v in (sb5_, rb5_, q5_, own5_, ra5_, rb5b_))
        sp, sb7, rb7, q7, own7, rr7, ct = (v.at[hf] for v in (sp_, sb7_, rb7_, q7_, own7_, rr7_, ct_))
        acc8, q8, rr8 = (v.at[hf] for v in (acc8_, q8_, rr8_))
        cols = pl.ds(hf * W, W)

        sib = {}
        need(0)
        xv = x_v[:, hf * W : (hf + 1) * W]
        ring = Sum(cm, "x", lambda d: q1.at[d], lambda i: rr1.at[i])
        for i, (away, d) in enumerate(order):
            need(1 + i)
            part = dot(a_v[a_rows(d, away), :], xv)
            if away:
                sb1[d] = part.astype(BF)
                if hf == 0 and i == 0:
                    pl.semaphore_wait(barrier, 34)
                sib[d] = cm.send(sb1.at[d], rb1.at[d], "c")
                continue
            sib[d].wait_recv()
            part = part + rb1[d].astype(F32)
            if d:
                q1[d] = part.astype(BF)
                ring.put(d)
            else:
                own1[...] = part
        yield
        if hf == 0:
            slot_tables()
        tot = ring.total(own1[...])
        y_v[x, k] = tot.astype(BF)

        fwd = {0: cm.send(y_v.at[x, k], y_v.at[x, k], "c")}
        gat = Gather(cm, "x", x, lambda i: y_v.at[i, k])
        yt[...] = tot.T.astype(BF)
        need(10)

        def push(xx, core, first=False):
            part = dot(b_v[:, panel_cols(xx, core)], y_v[xx, core])
            u_acc[...] = part if first else u_acc[...] + part

        push(x, k, True)
        yield
        fwd[0].wait_recv()
        push(x, 1 - k)
        yield
        at = {}
        for d in (1, 3, 2):
            at[d] = gat.wait(d)
            fwd[d] = cm.send(y_v.at[at[d], k], y_v.at[at[d], k], "c")
            push(at[d], k)
            if d == 1:
                continue
            last = 1 if d == 3 else 3
            fwd[last].wait_recv()
            push(at[last], 1 - k)
            yield
        fwd[2].wait_recv()
        push(at[2], 1 - k)

        for i in range(4):
            rows = u_acc[i * blk : (i + 1) * blk].astype(BF)
            g32[:, i * 8 : (i + 1) * 8, :] = dot(s1[i], rows).reshape(32, 8, W)
        g_v[...] = g32[...].astype(BF)
        plane_exchange(g_v, lambda to: to, r1_v, 1 + 2 * hf)
        r1_v[pl.ds(me, 1)] = g_v[pl.ds(me, 1)]
        yield
        if hf == 0:
            parent_tables()
        plane_wait(r1_v, 1 + 2 * hf)
        got = r1_v[0:8].astype(F32)
        for i in range(1, 4):
            got = got + r1_v[8 * i : 8 * i + 8].astype(F32)
        got = got.reshape(256, W).astype(BF)

        def t_rows(d):
            return t1[pl.ds(pl.multiple_of(((l + d) % 4) * own, own), own), :]

        ring = Sum(cm, "y", lambda d: q3.at[d], lambda i: rr3.at[i])
        for d in (2, 1, 3):
            q3[d] = dot(t_rows(d), got).astype(BF)
            ring.put(d)
        tot = dot(t_rows(0), got)
        yield
        need(9)
        tot = rp_v[:, hf * W : (hf + 1) * W].astype(F32) - ring.total(tot)
        gred[r, x, k] = tot.astype(BF)

        if hf == 0:
            gat = Gather(cm, "x", x, lambda i: gred.at[r, i, k])
        else:
            gat = Gather(cm, "z", r, lambda i: gred.at[i, x, k])
            for i in range(4):
                s1t[i] = s1[i].astype(F32).T.astype(BF)
        yield
        gat.run()
        if hf == 0:
            part = lambda i: gred.at[i, :, k]
            gat = Gather(cm, "z", r, part)
            mine = r
        else:
            part = lambda i: gred.at[:, i, k]
            gat = Gather(cm, "x", x, part)
            mine = x
        fwd = [cm.send(part(mine), part(mine), "c")]
        need(11)
        yield
        for d in (1, 3, 2):
            i = gat.wait(d)
            fwd.append(cm.send(part(i), part(i), "c"))
        yield
        for copy in fwd:
            copy.wait_recv()
        parent = dot(p_v[...], gred[...].reshape(32 * own, W))
        u_acc[: 4 * own] = parent

        def f_rows(d):
            return u_acc[pl.ds(pl.multiple_of(((l + d) % 4) * own, own), own), :]

        ring = Sum(cm, "y", lambda d: q4.at[d], lambda i: rr4.at[i])
        for d in (2, 1, 3):
            q4[d] = f_rows(d).astype(BF)
            ring.put(d)
        yield
        ft[l] = ring.total(f_rows(0)).T.astype(BF)
        gat = Gather(cm, "y", l, lambda i: ft.at[i])
        yield
        gat.run()

        lhs = jnp.concatenate([ft[i] for i in range(4)], axis=1)
        sib = {}
        for dr in (2, 3, 1, 0):
            for dx in range(4):
                block = ((r + dr) % 4) * 4 + (x + dx) % 4
                part = dot(lhs, p_v[:, pl.ds(pl.multiple_of(block * 2 * own, 2 * own), 2 * own)])
                lo, hi = part[:, :own], part[:, own:]
                own5[dr, dx] = jnp.where(k == 0, lo, hi)
                sb5[dr, dx] = jnp.where(k == 0, hi, lo).astype(BF)
            sib[dr] = cm.send(sb5.at[dr], rb5.at[dr], "c")
        yield
        if hf == 0:
            ring = Sum(cm, "z", lambda d: q5.at[d], lambda i: ra5.at[i])
        else:
            ring = Sum(cm, "x", lambda d: q5.at[:, d], lambda i: ra5.at[i])
        for dr in (2, 3, 1, 0):
            sib[dr].wait_recv()
            tot = own5[dr] + rb5[dr].astype(F32)
            own5[dr] = tot
            q5[dr] = tot.astype(BF)
            if dr and hf == 0:
                ring.put(dr)
        if hf == 1:
            ring.run()
        yield
        if hf == 0:
            tot = ring.total(own5[0])
            q5[0] = tot.astype(BF)
            ring = Sum(cm, "x", lambda d: q5.at[0, d], lambda i: rb5b.at[i])
        else:
            tot = ring.total(own5[:, 0])
            q5[:, 0] = tot.astype(BF)
            ring = Sum(cm, "z", lambda d: q5.at[d, 0], lambda i: rb5b.at[i])
        ring.run()
        yield
        solved = ring.total(tot[0]).T.astype(BF)
        sp[l] = solved

        gat = Gather(cm, "y", l, lambda i: sp.at[i])
        solp_ref[:, hf * W : (hf + 1) * W] = solved
        yield
        gat.run()
        g_v[0:8] = dot(t1t[...], sp[...].reshape(4 * own, W)).astype(BF).reshape(8, 32, W)
        plane_exchange(g_v, lambda to: to % 8, r2_v, 2 + 2 * hf)
        r2_v[pl.ds(me, 1)] = g_v[pl.ds(c, 1)]
        yield
        plane_wait(r2_v, 2 + 2 * hf)
        g32[...] = r2_v[...].astype(F32)
        picked = jnp.concatenate(
            [dot(s1t[i], g32[:, i * 8 : (i + 1) * 8, :].reshape(256, W).astype(BF)) for i in range(4)], axis=0
        )
        picked = picked.T.astype(BF)

        sib = {}
        ring = Sum(cm, "x", lambda d: q7.at[d], lambda i: rr7.at[i])
        for away, d in order:
            part = dot(picked, b_v[:, panel_cols((x + d) % 4, 1 - k if away else k)])
            if away:
                sb7[d] = part.astype(BF)
                sib[d] = cm.send(sb7.at[d], rb7.at[d], "c")
                continue
            sib[d].wait_recv()
            part = part + rb7[d].astype(F32)
            if d:
                q7[d] = part.astype(BF)
                ring.put(d)
            else:
                own7[...] = part
        yield
        tot = ring.total(own7[...])
        ct[x, k] = (yt[...].astype(F32) - tot).astype(BF)

        fwd = {0: cm.send(ct.at[x, k], ct.at[x, k], "c")}
        gat = Gather(cm, "x", x, lambda i: ct.at[i, k])
        ring = Sum(cm, "z", lambda d: q8.at[d], lambda i: rr8.at[i])

        def pull(xx, core, first=False, last=False):
            lhs = ct[xx, core]
            rows = pl.ds(pl.multiple_of((xx * 2 + core) * n8, n8), n8)
            for d in (2, 1, 3, 0):
                part = dot(lhs, a_v[rows, pl.ds(pl.multiple_of(((r + d) % 4) * n8, n8), n8)])
                part = part if first else acc8[d] + part
                if last and d:
                    q8[d] = part.astype(BF)
                    ring.put(d)
                else:
                    acc8[d] = part

        pull(x, k, True)
        yield
        fwd[0].wait_recv()
        pull(x, 1 - k)
        yield
        at = {}
        for d in (1, 3, 2):
            at[d] = gat.wait(d)
            fwd[d] = cm.send(ct.at[at[d], k], ct.at[at[d], k], "c")
            pull(at[d], k)
            if d == 1:
                continue
            last = 1 if d == 3 else 3
            fwd[last].wait_recv()
            pull(at[last], 1 - k)
            yield
        fwd[2].wait_recv()
        pull(at[2], 1 - k, last=True)
        yield
        out_ref[r, :, hf * W : (hf + 1) * W] = ring.total(acc8[0]).T.astype(BF)
        gat = Gather(cm, "z", r, lambda i: out_ref.at[i, :, cols])
        yield
        gat.run()

    halves = [chain(0), chain(1)]
    while halves:
        halves = [half for half in halves if next(half, True) is None]
    cm.drain()


def per_device(rhs_leaf, rhs_parent, inv_leaf, panel, row_map, inv_parent):
    rows, cols = inv_leaf.shape[1:]
    pb = panel.shape[1]
    R = rhs_leaf.shape[2]
    own = rhs_parent.shape[0]
    n8, blk, H = rows // 8, pb // 4, R // 2
    prow, pcol = inv_parent.shape
    V = pltpu.VMEM
    any_spec = pl.BlockSpec(memory_space=pl.ANY)
    vmem = pl.BlockSpec(memory_space=pltpu.VMEM)
    scratch = [
        V((rows, cols), BF), V((pb, rows), BF), V((prow, pcol), BF), V((cols, R), BF), V((own, R), BF),
        V((2, 4, n8, H), BF), V((2, 4, n8, H), BF), V((2, 4, n8, H), BF), V((2, n8, H), F32), V((2, 3, n8, H), BF),
        V((2, 4, 2, n8, H), BF), V((2, H, n8), BF),
        V((2, pb, H), F32), V((2, 32, 32, H), F32), V((2, 32, 32, H), BF), V((2, 32, 32, H), BF),
        V((2, 32, 32, H), BF), V((8, 32, own), F32), V((8, 32, own), F32),
        V((4 * own, 256), BF), V((256, 4 * own), BF), V((4, 256, blk), BF), V((4, blk, 256), BF),
        V((2, 4, own, H), BF), V((2, 3, own, H), BF), V((2, 4, 4, 2, own, H), BF),
        V((2, 4, own, H), BF), V((2, 3, own, H), BF), V((2, 4, H, own), BF),
        V((2, 4, 4, H, own), BF), V((2, 4, 4, H, own), BF), V((2, 4, 4, H, own), BF), V((2, 4, 4, H, own), F32),
        V((2, 3, 4, H, own), BF), V((2, 3, H, own), BF),
        V((2, 4, own, H), BF),
        V((2, 4, H, n8), BF), V((2, 4, H, n8), BF), V((2, 4, H, n8), BF), V((2, H, n8), F32), V((2, 3, H, n8), BF),
        V((2, 4, 2, H, n8), BF),
        V((2, 4, H, n8), F32), V((2, 4, H, n8), BF), V((2, 3, H, n8), BF),
        pltpu.SemaphoreType.DMA((160,)), pltpu.SemaphoreType.DMA((160,)), pltpu.SemaphoreType.DMA((12,)),
        pltpu.SemaphoreType.DMA((5,)), pltpu.SemaphoreType.DMA((5,)),
    ]
    sol_leaf, sol_parent = pl.pallas_call(
        kernel,
        out_shape=(
            jax.ShapeDtypeStruct((4, n8, R), BF),
            jax.ShapeDtypeStruct((own, R), BF),
        ),
        in_specs=[any_spec] * 5 + [vmem],
        out_specs=(vmem, vmem),
        scratch_shapes=scratch,
        compiler_params=pltpu.CompilerParams(
            collective_id=0, has_side_effects=True, vmem_limit_bytes=60 * 1024 * 1024
        ),
    )(
        rhs_leaf[0],
        rhs_parent,
        inv_leaf[0],
        panel[0],
        inv_parent,
        row_map[0].reshape(4, blk),
    )
    return (sol_leaf.reshape(1, 4 * n8, R), sol_parent)


def solution(mesh):
    in_specs = (
        P("leaf", "col", None),
        P(("leaf", "row", "col"), None),
        P("leaf", "row", "col"),
        P("leaf", "col", "row"),
        P("leaf", "col"),
        P(("row", "col"), "leaf"),
    )
    out_specs = (P("leaf", "col", None), P(("leaf", "row", "col"), None))
    return jax.shard_map(
        per_device, mesh=mesh, in_specs=in_specs, out_specs=out_specs, check_vma=False
    )
```

time: 729 us -> 153 us (0.21)
  waiting for transfers between devices: 383 us -> 0 us
  blocking collectives: 252 us -> 0 us
  Pallas kernels: 0 us -> 148 us
  matrix products: 35.8 us -> 0 us
  local copies, waits for them, and re-layouts: 21.7 us -> 4.21 us
  other arithmetic: 15.4 us -> 0.7 us
  between operations: 13.9 us -> 0.64 us
    psum x4 -> x0, blocking collectives: 252 us -> none  [the longest x1 148 us: per_device(): reduced = lax.psum(leaf_block, ('row', 'col')).astype(jnp.bfloat16)]
    reduce_scatter x2 -> x0, waiting for transfers between devices: 235 us -> none  [the longest x1 151 us: per_device(): lax.psum_scatter(dense, 'leaf', scatter_dimension=0, tiled=True)]
    pallas_call x0 -> x1, Pallas kernels: none -> 148 us  [per_device(): pl.pallas_call(kernel, out_shape=(jax.ShapeDtypeStruct((4, n8, R), BF), j...]
    all_gather x1 -> x0, waiting for transfers between devices: 82.3 us -> none  [per_device(): lax.all_gather(sol_parent, ('leaf', 'row', 'col'), axis=0, tiled=True)]
    psum x1 -> x0, waiting for transfers between devices: 65.8 us -> none  [per_device(): coupling = lax.psum(coupling_part, 'col')]
    dot_general x6 -> x0, matrix products: 35.8 us -> none  [the longest x1 8.46 us: per_device(): lax.dot_general(inv_leaf[0], corrected, (((0,), (0,)), ((), ())), preferr...]
    scatter-add x1 -> x0, other arithmetic: 12.3 us -> none  [dense_updates(): dense = dense.at[row_map[0]].add(-update)]
    all_gather x1 -> x0, local copies, waits for them, and re-layouts: 11.9 us -> none  [per_device(): lax.all_gather(sol_parent, ('leaf', 'row', 'col'), axis=0, tiled=True)]
  transfers between devices with their start and end apart: 4 -> 0, of which waited for: 4 -> 0; matrix products, arithmetic and copies ran while one was open for 0% -> 0% of each run, Pallas kernels for 0% -> 0%
where the time goes in v3:
time: 153 us
  Pallas kernels  148 us (97%)
  local copies, waits for them, and re-layouts  4.21 us (3%)
    pallas_call x1, Pallas kernels, per_device(): pl.pallas_call(kernel, out_shape=(jax.ShapeDtypeStruct((4, n8, R), BF), j...  148 us
    unnamed x2, local copies, waits for them, and re-layouts  3.54 us

profile of v3, /device:TPU:1, one launch (start us, length us, event | category | flops | bytes accessed | tf_op | source)
XLA Modules:
  0.0 153.2 jit_solution(2222462022311432052)
XLA Ops:
  0.6 0.7 reduce
  1.3 0.7 reshape_squeeze.3.rm_ref
  2.0 147.7 %shard_map.77 = (bf16[4,384,256]{2,1,0:T(8,128)(2,1)}, bf16[128,256]{1,0:T(8,128)(2,1)}) custom-call(bf16[1536,256]{1,0:T(8,128)(2,1)} %bitcast.7, bf16[128,256]{1,0:T(8,128)(2,1)} %rp_hbm.1, bf16[3072,1536]{1,0:T(8,128)(2,1)} %bitcast.4, bf16[768,3072]{1,0:T(8,128)(2,1)} %bitcast.5, bf16[512,4096]{1,0:T(8,128)(2,1)} %p_hbm.1, s32[4,192]{1,0:T(4,128)} %reshape_squeeze.3.rm_ref), custom_call_target="tpu_custom_call" | custom-call | tf_op jit(solution)/shard_map/pallas_call | solution.py:489
  149.7 2.1 %copy.10 = bf16[1,1536,256]{2,1,0:T(8,128)(2,1)} copy(bf16[1,1536,256]{2,1,0:T(8,128)(2,1)} %bitcast.6) | data formatting | bytes 1572864
  151.7 1.5 copy.11

commit v4 on v3

--- a/solution.py
+++ b/solution.py
@@ -171,7 +171,7 @@
         shift = own.bit_length() - 1
         before = lax.broadcasted_iota(jnp.int32, (blk, blk), 0) < lax.broadcasted_iota(jnp.int32, (blk, blk), 1)
         for i in range(4):
-            e = rm_ref[i : i + 1, :]
+            e = rm_ref[0:1, i * blk : (i + 1) * blk]
             owner = lax.shift_right_logical(e, shift)
             local = lax.bitwise_and(e, own - 1).astype(F32)
             across = jnp.broadcast_to(owner.astype(F32), (blk, blk))
@@ -238,8 +238,6 @@
             else:
                 own1[...] = part
         yield
-        if hf == 0:
-            slot_tables()
         tot = ring.total(own1[...])
         y_v[x, k] = tot.astype(BF)
 
@@ -254,22 +252,19 @@
 
         push(x, k, True)
         yield
+        if hf == 0:
+            slot_tables()
         fwd[0].wait_recv()
         push(x, 1 - k)
-        yield
         at = {}
         for d in (1, 3, 2):
             at[d] = gat.wait(d)
             fwd[d] = cm.send(y_v.at[at[d], k], y_v.at[at[d], k], "c")
+        for d in (1, 3, 2):
             push(at[d], k)
-            if d == 1:
-                continue
-            last = 1 if d == 3 else 3
-            fwd[last].wait_recv()
-            push(at[last], 1 - k)
-            yield
-        fwd[2].wait_recv()
-        push(at[2], 1 - k)
+        for d in (1, 3, 2):
+            fwd[d].wait_recv()
+            push(at[d], 1 - k)
 
         for i in range(4):
             rows = u_acc[i * blk : (i + 1) * blk].astype(BF)
@@ -350,7 +345,6 @@
                 own5[dr, dx] = jnp.where(k == 0, lo, hi)
                 sb5[dr, dx] = jnp.where(k == 0, hi, lo).astype(BF)
             sib[dr] = cm.send(sb5.at[dr], rb5.at[dr], "c")
-        yield
         if hf == 0:
             ring = Sum(cm, "z", lambda d: q5.at[d], lambda i: ra5.at[i])
         else:
@@ -432,20 +426,15 @@
         yield
         fwd[0].wait_recv()
         pull(x, 1 - k)
-        yield
         at = {}
         for d in (1, 3, 2):
             at[d] = gat.wait(d)
             fwd[d] = cm.send(ct.at[at[d], k], ct.at[at[d], k], "c")
+        for d in (1, 3, 2):
             pull(at[d], k)
-            if d == 1:
-                continue
-            last = 1 if d == 3 else 3
-            fwd[last].wait_recv()
-            pull(at[last], 1 - k)
-            yield
-        fwd[2].wait_recv()
-        pull(at[2], 1 - k, last=True)
+        for d in (1, 3, 2):
+            fwd[d].wait_recv()
+            pull(at[d], 1 - k, last=d == 2)
         yield
         out_ref[r, :, hf * W : (hf + 1) * W] = ring.total(acc8[0]).T.astype(BF)
         gat = Gather(cm, "z", r, lambda i: out_ref.at[i, :, cols])
@@ -504,7 +493,7 @@
         inv_leaf[0],
         panel[0],
         inv_parent,
-        row_map[0].reshape(4, blk),
+        row_map,
     )
     return (sol_leaf.reshape(1, 4 * n8, R), sol_parent)
 

time: 153 us -> 143 us (0.935)
  Pallas kernels: 148 us -> 139 us
    pallas_call x1, Pallas kernels: 148 us -> 139 us  [per_device(): pl.pallas_call(kernel, out_shape=(jax.ShapeDtypeStruct((4, n8, R), BF), j...]
where the time goes in v4:
time: 143 us
  Pallas kernels  139 us (97%)
  local copies, waits for them, and re-layouts  3.54 us (2%)
    pallas_call x1, Pallas kernels, per_device(): pl.pallas_call(kernel, out_shape=(jax.ShapeDtypeStruct((4, n8, R), BF), j...  139 us
    unnamed x2, local copies, waits for them, and re-layouts  3.54 us

profile of v4, /device:TPU:1, one launch (start us, length us, event | category | flops | bytes accessed | tf_op | source)
XLA Modules:
  0.0 143.1 jit_solution(8321026108261440988)
XLA Ops:
  0.6 138.9 %shard_map.77 = (bf16[4,384,256]{2,1,0:T(8,128)(2,1)}, bf16[128,256]{1,0:T(8,128)(2,1)}) custom-call(bf16[1536,256]{1,0:T(8,128)(2,1)} %bitcast.6, bf16[128,256]{1,0:T(8,128)(2,1)} %rp_hbm.1, bf16[3072,1536]{1,0:T(8,128)(2,1)} %bitcast.4, bf16[768,3072]{1,0:T(8,128)(2,1)} %bitcast.5, bf16[512,4096]{1,0:T(8,128)(2,1)} %p_hbm.1, s32[1,768]{1,0:T(1,128)} %rm_ref.1), custom_call_target="tpu_custom_call" | custom-call | tf_op jit(solution)/shard_map/pallas_call | solution.py:478
  139.5 2.1 %copy.10 = bf16[1,1536,256]{2,1,0:T(8,128)(2,1)} copy(bf16[1,1536,256]{2,1,0:T(8,128)(2,1)} %bitcast.7) | data formatting | bytes 1572864
  141.6 1.5 %copy.11 = bf16[128,256]{1,0:T(8,128)(2,1)} copy(bf16[128,256]{1,0:T(8,128)(2,1)} %get-tuple-element.9) | data formatting | bytes 131072

commit v5 on v4

--- a/solution.py
+++ b/solution.py
@@ -61,7 +61,7 @@
         self.copies[d] = self.comm.send(self.q(d), self.slot(d - 1), self.axis, d)
 
     def run(self):
-        for d in (2, 1, 3):
+        for d in (1, 3, 2):
             self.put(d)
 
     def total(self, own):
@@ -74,7 +74,7 @@
 class Gather:
     def __init__(self, comm, axis, me, g):
         self.me = me
-        self.copies = {d: comm.send(g(me), g(me), axis, d) for d in (2, 1, 3)}
+        self.copies = {d: comm.send(g(me), g(me), axis, d) for d in (1, 3, 2)}
 
     def wait(self, d):
         self.copies[d].wait_recv()
@@ -104,7 +104,7 @@
     W = x_v.shape[1] // 2
     own = rp_v.shape[0]
     blk = s1t.shape[1]
-    order = ((1, 2), (1, 3), (0, 2), (1, 1), (0, 3), (1, 0), (0, 1), (0, 0))
+    order = ((1, 2), (1, 3), (1, 1), (1, 0), (0, 2), (0, 3), (0, 1), (0, 0))
 
     def a_rows(d, away):
         core = 1 - k if away else k

time: 143 us -> 140 us (0.979)
  Pallas kernels: 139 us -> 136 us
    pallas_call x1, Pallas kernels: 139 us -> 136 us  [per_device(): pl.pallas_call(kernel, out_shape=(jax.ShapeDtypeStruct((4, n8, R), BF), j...]
where the time goes in v5:
time: 140 us
  Pallas kernels  136 us (97%)
  local copies, waits for them, and re-layouts  3.54 us (3%)
    pallas_call x1, Pallas kernels, per_device(): pl.pallas_call(kernel, out_shape=(jax.ShapeDtypeStruct((4, n8, R), BF), j...  136 us
    unnamed x2, local copies, waits for them, and re-layouts  3.54 us

profile of v5, /device:TPU:1, one launch (start us, length us, event | category | flops | bytes accessed | tf_op | source)
XLA Modules:
  0.0 140.2 jit_solution(3369998280617452962)
XLA Ops:
  0.6 136.0 %shard_map.77 = (bf16[4,384,256]{2,1,0:T(8,128)(2,1)}, bf16[128,256]{1,0:T(8,128)(2,1)}) custom-call(bf16[1536,256]{1,0:T(8,128)(2,1)} %bitcast.6, bf16[128,256]{1,0:T(8,128)(2,1)} %rp_hbm.1, bf16[3072,1536]{1,0:T(8,128)(2,1)} %bitcast.4, bf16[768,3072]{1,0:T(8,128)(2,1)} %bitcast.5, bf16[512,4096]{1,0:T(8,128)(2,1)} %p_hbm.1, s32[1,768]{1,0:T(1,128)} %rm_ref.1), custom_call_target="tpu_custom_call" | custom-call | tf_op jit(solution)/shard_map/pallas_call | solution.py:478
  136.6 2.1 %copy.10 = bf16[1,1536,256]{2,1,0:T(8,128)(2,1)} copy(bf16[1,1536,256]{2,1,0:T(8,128)(2,1)} %bitcast.7) | data formatting | bytes 1572864
  138.7 1.5 %copy.11 = bf16[128,256]{1,0:T(8,128)(2,1)} copy(bf16[128,256]{1,0:T(8,128)(2,1)} %get-tuple-element.9) | data formatting | bytes 131072

commit v6 on v5

--- a/solution.py
+++ b/solution.py
@@ -184,6 +184,7 @@
                 0.0,
             )
             s1[i] = pick.astype(BF)
+            s1t[i] = pick.T.astype(BF)
             near = (lax.broadcasted_iota(jnp.int32, (64, blk), 0) + r * 64).astype(F32)
             where = jnp.where(near == jnp.broadcast_to(place, (64, blk)), jnp.broadcast_to(local + 1.0, (64, blk)), 0.0)
             qv = jnp.sum(where, axis=1, keepdims=True)
@@ -243,17 +244,17 @@
 
         fwd = {0: cm.send(y_v.at[x, k], y_v.at[x, k], "c")}
         gat = Gather(cm, "x", x, lambda i: y_v.at[i, k])
-        yt[...] = tot.T.astype(BF)
         need(10)
 
         def push(xx, core, first=False):
             part = dot(b_v[:, panel_cols(xx, core)], y_v[xx, core])
             u_acc[...] = part if first else u_acc[...] + part
 
-        push(x, k, True)
         yield
         if hf == 0:
             slot_tables()
+        yt[...] = tot.T.astype(BF)
+        push(x, k, True)
         fwd[0].wait_recv()
         push(x, 1 - k)
         at = {}
@@ -298,8 +299,6 @@
             gat = Gather(cm, "x", x, lambda i: gred.at[r, i, k])
         else:
             gat = Gather(cm, "z", r, lambda i: gred.at[i, x, k])
-            for i in range(4):
-                s1t[i] = s1[i].astype(F32).T.astype(BF)
         yield
         gat.run()
         if hf == 0:
@@ -373,8 +372,8 @@
         sp[l] = solved
 
         gat = Gather(cm, "y", l, lambda i: sp.at[i])
+        yield
         solp_ref[:, hf * W : (hf + 1) * W] = solved
-        yield
         gat.run()
         g_v[0:8] = dot(t1t[...], sp[...].reshape(4 * own, W)).astype(BF).reshape(8, 32, W)
         plane_exchange(g_v, lambda to: to % 8, r2_v, 2 + 2 * hf)
@@ -422,8 +421,8 @@
                 else:
                     acc8[d] = part
 
+        yield
         pull(x, k, True)
-        yield
         fwd[0].wait_recv()
         pull(x, 1 - k)
         at = {}

time: 140 us -> 140 us (level)
  no operation moved by 1% of the time
where the time goes in v6:
time: 140 us
  Pallas kernels  136 us (97%)
  local copies, waits for them, and re-layouts  3.54 us (3%)
    pallas_call x1, Pallas kernels, per_device(): pl.pallas_call(kernel, out_shape=(jax.ShapeDtypeStruct((4, n8, R), BF), j...  136 us
    unnamed x2, local copies, waits for them, and re-layouts  3.54 us

profile of v6, /device:TPU:1, one launch (start us, length us, event | category | flops | bytes accessed | tf_op | source)
XLA Modules:
  0.0 139.8 jit_solution(14858094136585649625)
XLA Ops:
  0.6 135.7 %shard_map.77 = (bf16[4,384,256]{2,1,0:T(8,128)(2,1)}, bf16[128,256]{1,0:T(8,128)(2,1)}) custom-call(bf16[1536,256]{1,0:T(8,128)(2,1)} %bitcast.6, bf16[128,256]{1,0:T(8,128)(2,1)} %rp_hbm.1, bf16[3072,1536]{1,0:T(8,128)(2,1)} %bitcast.4, bf16[768,3072]{1,0:T(8,128)(2,1)} %bitcast.5, bf16[512,4096]{1,0:T(8,128)(2,1)} %p_hbm.1, s32[1,768]{1,0:T(1,128)} %rm_ref.1), custom_call_target="tpu_custom_call" | custom-call | tf_op jit(solution)/shard_map/pallas_call | solution.py:477
  136.3 2.1 %copy.10 = bf16[1,1536,256]{2,1,0:T(8,128)(2,1)} copy(bf16[1,1536,256]{2,1,0:T(8,128)(2,1)} %bitcast.7) | data formatting | bytes 1572864
  138.4 1.5 %copy.11 = bf16[128,256]{1,0:T(8,128)(2,1)} copy(bf16[128,256]{1,0:T(8,128)(2,1)} %get-tuple-element.9) | data formatting | bytes 131072
